TPU v7x, 128 devices: a whole 4x4x4 slice. The times are simulated.
128 devices in a mesh: row: 16 (over y, x), col: 8 (over z, core).
Axes of the slice: x: 4, y: 4, z: 4, core: 2. Of those that a mesh axis runs over, the one named last changes fastest.
Arguments:
- orbitals: float32 [32768, 1024], P('row', 'col'), may hold values from -6 to 6
- point_index: int32 [8192], replicated, may hold values from 0 to 32767, as said below
- coulomb: float32 [8192, 8192], P('row', 'col'), may hold values from -0.001953125 to 0.001953125
- fitting: float32 [32768, 8192], P('row', 'col'), may hold values from -0.0625 to 0.0625
Outputs:
- exchange_out: float32 [32768, 1024], P('row', 'col')
Inputs may be any that keep to these rules, and one draw needn't show every extreme that they name: `point_index`: indices are distinct. Grid index g lies in slab g // 2048. Of the 512 consecutive points of each row panel, at most 64 lie in one slab, and in every panel exactly 64 lie in one slab.
All inputs are finite; a program needn't handle non-finite values.
Results may differ from a plain program's by a relative error of at most 0.00012.
Values sent between devices are 32-bit elements; how exact they have to be, the bound alone decides.
No kernel may reach another device: no remote copies, remote signals or barrier semaphores. Data moves between devices by JAX's collectives and lax.ppermute only.
A program may use at most 64 MiB of HBM per device.

v0:
```python
import jax
import jax.numpy as jnp
from jax import lax
from jax.sharding import PartitionSpec as P


def per_device(orbitals, point_index, coulomb, fitting):
    row_count = lax.axis_size("row")
    slab_rows = orbitals.shape[0]
    band_cols = orbitals.shape[1]
    total_points = point_index.shape[0]
    per_panel = total_points // row_count
    slot_count = 2 * per_panel // row_count
    my_row = lax.axis_index("row")
    my_col = lax.axis_index("col")
    owner = point_index // slab_rows
    local_row = point_index - owner * slab_rows
    owner_grid = owner.reshape(row_count, per_panel)
    local_grid = local_row.reshape(row_count, per_panel)
    matches = (owner_grid[:, :, None] == jnp.arange(row_count)[None, None, :]).astype(jnp.int32)
    ranking = jnp.cumsum(matches, axis=1) - 1
    slot_grid = jnp.sum(jnp.where(matches > 0, ranking, 0), axis=2)
    mine = owner_grid == my_row
    chosen = mine[:, :, None] & (slot_grid[:, :, None] == jnp.arange(slot_count)[None, None, :])
    source_row = jnp.sum(jnp.where(chosen, local_grid[:, :, None], 0), axis=1)
    valid = jnp.any(chosen, axis=1)
    outgoing = jnp.where(valid[:, :, None], orbitals[source_row], 0.0)
    received = lax.all_to_all(outgoing, "row", split_axis=0, concat_axis=0, tiled=True)
    flattened = received.reshape(row_count * slot_count, band_cols)
    owner_mine = lax.dynamic_slice_in_dim(owner_grid, my_row, 1, 0)[0]
    slot_mine = lax.dynamic_slice_in_dim(slot_grid, my_row, 1, 0)[0]
    panel_strip = flattened[owner_mine * slot_count + slot_mine]
    panel_full = lax.all_gather(panel_strip, "col", axis=1, tiled=True)
    strip_all = lax.all_gather(panel_strip, "row", axis=0, tiled=True)
    column_full = lax.all_to_all(strip_all, "col", split_axis=0, concat_axis=1, tiled=True)
    pair = jnp.dot(
        panel_full,
        column_full.T,
        precision=lax.Precision.HIGHEST,
        preferred_element_type=jnp.float32,
    )
    partial_value = jnp.dot(
        coulomb * pair,
        column_full,
        precision=lax.Precision.HIGHEST,
        preferred_element_type=jnp.float32,
    )
    summed = lax.psum(partial_value, "col")
    weight_strip = lax.dynamic_slice_in_dim(summed, my_col * band_cols, band_cols, 1)
    weight_all = lax.all_gather(weight_strip, "row", axis=0, tiled=True)
    weight_column = lax.all_to_all(weight_all, "col", split_axis=0, concat_axis=1, tiled=True)
    term = -jnp.dot(
        fitting, weight_column, precision=lax.Precision.HIGHEST, preferred_element_type=jnp.float32
    )
    return lax.psum_scatter(term, "col", scatter_dimension=1, tiled=True)


def solution(mesh):
    in_specs = (P("row", "col"), P(), P("row", "col"), P("row", "col"))
    out_specs = P("row", "col")
    return jax.shard_map(
        per_device, mesh=mesh, in_specs=in_specs, out_specs=out_specs, check_vma=False
    )
```

profile of v0, /device:TPU:1, one launch (start us, length us, event | category | flops | bytes accessed | tf_op | source)
XLA Modules:
  0.0 455.0 jit_solution(17053227646644260959)
XLA Ops:
  6.5 0.0 copy-start
  6.5 0.9 add_select_fusion
  7.4 0.1 fusion.6
  7.5 18.1 %reduce-window.6 = s32[16,16,4,128]{3,1,2,0:T(8,128)S(1)} reduce-window(s32[16,16,4,128]{3,1,2,0:T(8,128)S(1)} %fusion.6, s32[]{:T(128)} %constant.16.clone.1), window={size=1x1x1x128 pad=0_0x0_0x0_0x127_0}, to_apply=%region_0.1 | reduce-window | flops 16646144 | bytes 1048580 | tf_op jit(solution)/shard_map/reduce-window
  25.6 0.2 slice.12
  25.9 0.4 copy.12
  26.3 0.1 fusion.8
  26.5 0.2 fusion.5
  26.7 0.4 fusion.3
  27.1 0.5 select_reduce_fusion
  27.7 0.1 reshape.84
  27.7 0.0 copy-done
  27.7 2.8 gather_fusion
  30.6 1.0 broadcast_select_fusion
  31.5 7.6 %all-to-all-start = ((f32[16,64,128]{2,1,0:T(8,128)}), f32[16,64,128]{2,1,0:T(8,128)S(1)}, u32[]{:S(2)}, u32[]{:S(2)}) async-start(f32[16,64,128]{2,1,0:T(8,128)} %broadcast_select_fusion), calls=%async_computation | async-start | bytes 1048576 | tf_op jit(solution)/shard_map/all_to_all | solution.py:28
  39.1 0.0 all-gather.10.cloned.1.call-start
  39.2 10.3 %all-to-all-done = f32[16,64,128]{2,1,0:T(8,128)S(1)} async-done(((f32[16,64,128]{2,1,0:T(8,128)}), f32[16,64,128]{2,1,0:T(8,128)S(1)}, u32[]{:S(2)}, u32[]{:S(2)}) %all-to-all-start) | async-done | bytes 524320 | tf_op jit(solution)/shard_map/all_to_all | solution.py:28
  49.6 1.6 gather_fusion.1
  51.2 0.0 all-gather.10.cloned.1.call-update
  51.2 0.0 all-gather.8.cloned.1.call-start
  51.3 0.7 all-gather.8.cloned.1.call-update
  52.0 50.4 %all-gather.10.cloned.1.call-done = f32[8192,128]{1,0:T(8,128)} async-done(((f32[512,128]{1,0:T(8,128)}), f32[8192,128]{1,0:T(8,128)}) %all-gather.10.cloned.1.call-update) | async-done | bytes 4194320 | tf_op jit(solution)/shard_map/all_gather | solution.py:34
  102.4 5.4 %copy.15 = f32[8,1024,128]{1,2,0:T(8,128)} copy(f32[8,1024,128]{2,1,0:T(8,128)} %bitcast.44) | data formatting | bytes 8388608 | tf_op jit(solution)/shard_map/all_to_all | solution.py:35
  107.7 5.3 %all-to-all-start.1 = ((f32[8,1024,128]{1,2,0:T(8,128)}), f32[8,1024,128]{1,2,0:T(8,128)}, u32[]{:S(2)}, u32[]{:S(2)}) async-start(f32[8,1024,128]{1,2,0:T(8,128)} %copy.15), calls=%async_computation.1 | async-start | bytes 8388608 | tf_op jit(solution)/shard_map/all_to_all | solution.py:35
  113.0 0.0 all-reduce.2.cloned.1.call-start
  113.0 31.5 %all-gather.8.cloned.1.call-done = f32[512,1024]{1,0:T(8,128)} async-done(((f32[512,128]{1,0:T(8,128)}), f32[512,1024]{1,0:T(8,128)}) %all-gather.8.cloned.1.call-update) | async-done | bytes 2097168 | tf_op jit(solution)/shard_map/all_gather | solution.py:33
  144.5 25.7 %all-to-all-done.1 = f32[8,1024,128]{1,2,0:T(8,128)} async-done(((f32[8,1024,128]{1,2,0:T(8,128)}), f32[8,1024,128]{1,2,0:T(8,128)}, u32[]{:S(2)}, u32[]{:S(2)}) %all-to-all-start.1) | async-done | bytes 4194336 | tf_op jit(solution)/shard_map/all_to_all | solution.py:35
  170.2 0.0 copy-start.1
  170.2 9.8 %fusion.11 = f32[512,1024]{1,0:T(8,128)S(1)} fusion(f32[512,1024]{1,0:T(8,128)} %all-gather.8.cloned.1.call-done, f32[1024,1024]{0,1:T(8,128)} %bitcast.10), kind=kOutput, calls=%fused_computation.34 | convolution fusion | flops 6442450944 | bytes 8388608 | tf_op jit(solution)/shard_map/dot_general | solution.py:36
  180.0 0.0 copy-done.1
  180.0 9.8 %fusion = f32[512,1024]{1,0:T(8,128)} fusion(f32[1024,1024]{0,1:T(8,128)} %bitcast.10, f32[512,1024]{1,0:T(8,128)S(1)} %copy-done.1, f32[512,1024]{1,0:T(8,128)S(1)} %fusion.11), kind=kOutput, calls=%fused_computation.3 | convolution fusion | flops 6442975232 | bytes 10485760 | tf_op jit(solution)/shard_map/dot_general | solution.py:42
  189.8 0.0 all-reduce.2.cloned.1.call-update
  189.8 0.0 all-gather.6.cloned.1.call-start
  189.9 62.2 %all-reduce.2.cloned.1.call-done = f32[512,1024]{1,0:T(8,128)} async-done(((f32[512,1024]{1,0:T(8,128)}), f32[512,1024]{1,0:T(8,128)}) %all-reduce.2.cloned.1.call-update) | async-done | bytes 2097168 | tf_op jit(solution)/shard_map/psum | solution.py:48
  252.1 1.7 constant_dynamic-slice_fusion
  253.7 0.0 all-gather.6.cloned.1.call-update
  253.8 0.0 reduce-scatter.2.cloned.1.call-start
  253.8 52.7 %all-gather.6.cloned.1.call-done = f32[8192,128]{1,0:T(8,128)} async-done(((f32[512,128]{1,0:T(8,128)}), f32[8192,128]{1,0:T(8,128)}) %all-gather.6.cloned.1.call-update) | async-done | bytes 4194320 | tf_op jit(solution)/shard_map/all_gather | solution.py:50
  306.5 5.4 %copy.16 = f32[8,1024,128]{1,2,0:T(8,128)} copy(f32[8,1024,128]{2,1,0:T(8,128)} %bitcast.45) | data formatting | bytes 8388608 | tf_op jit(solution)/shard_map/all_to_all | solution.py:51
  311.9 53.9 %all_to_all.43 = f32[8,1024,128]{1,2,0:T(8,128)S(1)} all-to-all(f32[8,1024,128]{1,2,0:T(8,128)} %copy.16), channel_id=1, replica_groups=mesh['row'=16,'col'=8] {'col'}, dimensions={0} | all-to-all | bytes 8388608 | tf_op jit(solution)/shard_map/all_to_all | solution.py:51
  365.8 29.8 %negate_bitcast_fusion = f32[2048,1024]{0,1:T(8,128)} fusion(f32[1024,1024]{0,1:T(8,128)S(1)} %bitcast.46, f32[2048,1024]{1,0:T(8,128)} %param.7), kind=kOutput, calls=%fused_computation.2 | convolution fusion | flops 25771900928 | bytes 20971520 | tf_op jit(solution)/shard_map/dot_general | solution.py:52
  395.6 0.0 reduce-scatter.2.cloned.1.call-update
  395.7 50.2 %reduce-scatter.2.cloned.1.call-done = f32[2048,128]{0,1:T(8,128)} async-done(((f32[2048,1024]{0,1:T(8,128)}), f32[2048,128]{0,1:T(8,128)}) %reduce-scatter.2.cloned.1.call-update) | async-done | bytes 1048592 | tf_op jit(solution)/shard_map/reduce_scatter | solution.py:55
  445.9 2.5 copy.17
  (9 shorter events, 0.1 us)
Async XLA Ops:
  6.5 21.2 %copy-start = (f32[2048,128]{1,0:T(8,128)S(1)}, f32[2048,128]{1,0:T(8,128)}, u32[]{:S(2)}) copy-start(f32[2048,128]{1,0:T(8,128)} %param.4) | copy-start | bytes 3145732
  31.5 18.0 %all-to-all-start = ((f32[16,64,128]{2,1,0:T(8,128)}), f32[16,64,128]{2,1,0:T(8,128)S(1)}, u32[]{:S(2)}, u32[]{:S(2)}) async-start(f32[16,64,128]{2,1,0:T(8,128)} %broadcast_select_fusion), calls=%async_computation | async-start | bytes 1048576 | tf_op jit(solution)/shard_map/all_to_all | solution.py:28
  39.1 63.2 %all-gather.10.cloned.1.call-start = ((), (), s32[]{:S(2)}) async-start(), calls=%async_computation.8 | async-start | bytes 4456448 | tf_op jit(solution)/shard_map/all_gather | solution.py:34
  51.2 93.3 %all-gather.8.cloned.1.call-start = ((), (), s32[]{:S(2)}) async-start(), calls=%async_computation.7 | async-start | bytes 2359296 | tf_op jit(solution)/shard_map/all_gather | solution.py:33
  107.7 62.5 %all-to-all-start.1 = ((f32[8,1024,128]{1,2,0:T(8,128)}), f32[8,1024,128]{1,2,0:T(8,128)}, u32[]{:S(2)}, u32[]{:S(2)}) async-start(f32[8,1024,128]{1,2,0:T(8,128)} %copy.15), calls=%async_computation.1 | async-start | bytes 8388608 | tf_op jit(solution)/shard_map/all_to_all | solution.py:35
  113.0 139.1 %all-reduce.2.cloned.1.call-start = ((), (), s32[]{:S(2)}) async-start(), calls=%async_computation.4 | async-start | bytes 4194304 | tf_op jit(solution)/shard_map/psum | solution.py:48
  170.2 9.8 %copy-start.1 = (f32[512,1024]{1,0:T(8,128)S(1)}, f32[512,1024]{1,0:T(8,128)}, u32[]{:S(2)}) copy-start(f32[512,1024]{1,0:T(8,128)} %param.6) | copy-start | bytes 6291460
  189.8 116.7 %all-gather.6.cloned.1.call-start = ((), (), s32[]{:S(2)}) async-start(), calls=%async_computation.5 | async-start | bytes 4456448 | tf_op jit(solution)/shard_map/all_gather | solution.py:50
  253.8 192.1 %reduce-scatter.2.cloned.1.call-start = ((), (), s32[]{:S(2)}) async-start(), calls=%async_computation.6 | async-start | bytes 9437184 | tf_op jit(solution)/shard_map/reduce_scatter | solution.py:55
Sparse Core Ops, SparseCore 0:
  51.3 50.9 all-gather.9
  104.0 40.3 all-gather.7
  190.0 62.0 all-reduce.1
  254.1 52.4 all-gather.5
  395.8 50.0 reduce-scatter.1
where the time goes:
time: 456 us; the launch traced here: 455 us
  waiting for transfers between devices  284 us (62%)
  blocking collectives  53.9 us (12%)
  matrix products  49.4 us (11%)
  other arithmetic  21.4 us (5%)
  local copies, waits for them, and re-layouts  20.1 us (4%)
  between operations  13.3 us (3%)
  starting transfers between devices  13 us (3%)
    psum x1, waiting for transfers between devices, per_device(): summed = lax.psum(partial_value, 'col')  62.2 us
    all_to_all x1, blocking collectives, per_device(): lax.all_to_all(weight_all, 'col', split_axis=0, concat_axis=1, tiled=True)  53.9 us
    all_gather x1, waiting for transfers between devices, per_device(): weight_all = lax.all_gather(weight_strip, 'row', axis=0, tiled=True)  52.7 us
    all_gather x1, waiting for transfers between devices, per_device(): strip_all = lax.all_gather(panel_strip, 'row', axis=0, tiled=True)  50.4 us
    reduce_scatter x1, waiting for transfers between devices, per_device(): return lax.psum_scatter(term, 'col', scatter_dimension=1, tiled=True)  50.2 us
    all_gather x1, waiting for transfers between devices, per_device(): panel_full = lax.all_gather(panel_strip, 'col', axis=1, tiled=True)  31.5 us
    dot_general x1, matrix products, per_device(): jnp.dot(fitting, weight_column, precision=lax.Precision.HIGHEST, preferre...  29.8 us
    all_to_all x1, waiting for transfers between devices, per_device(): lax.all_to_all(strip_all, 'col', split_axis=0, concat_axis=1, tiled=True)  25.7 us
  transfers between devices with their start and end apart: 7, of which 7 were waited for; matrix products, arithmetic and copies ran while one was open for 1% of the time, Pallas kernels for 0%

commit v1 on v0

v1 whole, which is shorter than its diff:
```python
import functools

import jax
import jax.numpy as jnp
from jax import lax
from jax.experimental import pallas as pl
from jax.experimental.pallas import tpu as pltpu
from jax.sharding import PartitionSpec as P


SIDE = 4
REL = (0, -1, 1, 2)
F32 = jnp.float32
BF16 = jnp.bfloat16


def shift(axis, step):
    pairs = []
    if axis == "z":
        for z in range(SIDE):
            for k in range(2):
                pairs.append((z * 2 + k, ((z + step) % SIDE) * 2 + k))
        return "col", pairs
    for y in range(SIDE):
        for x in range(SIDE):
            ty = (y + step) % SIDE if axis == "y" else y
            tx = (x + step) % SIDE if axis == "x" else x
            pairs.append((y * SIDE + x, ty * SIDE + tx))
    return "row", pairs


def move(value, axis, step):
    name, pairs = shift(axis, step)
    return lax.ppermute(value, name, pairs)


def swap_cores(value):
    return lax.ppermute(value, "col", [(c, c ^ 1) for c in range(2 * SIDE)])


def scatter_pairs(turn):
    pairs = []
    for y in range(SIDE):
        for x in range(SIDE):
            for z in range(SIDE):
                for k in range(2):
                    strip = (z + turn) % SIDE
                    ty = (strip - y) % SIDE
                    tx = x if k == 0 else x ^ 3
                    target = (ty * SIDE + tx) * 8 + y * 2 + (x >> 1)
                    pairs.append(((y * SIDE + x) * 8 + z * 2 + k, target))
    return pairs


def to_plane(value, turn):
    return lax.ppermute(value, ("row", "col"), scatter_pairs(turn))


def gather_line(block, axis):
    half = block.shape[0] // 2
    before = move(block, axis, 1)
    after = move(block, axis, -1)
    far_low = move(before[:half], axis, 1)
    far_high = move(after[half:], axis, -1)
    return block, before, after, far_low, far_high


def gather_plane(block):
    half = block.shape[0] // 2
    first = gather_line(block[:half], "x")
    second = gather_line(block[half:], "y")
    shape = (SIDE, half) + block.shape[1:]
    first = jnp.concatenate(first, axis=0).reshape(shape)
    second = jnp.concatenate(second, axis=0).reshape(shape)
    return gather_line(first, "y") + gather_line(second, "x")


def plane_order(my_row, my_col):
    rel = jnp.array(REL, jnp.int32)
    y, x = my_row // SIDE, my_row % SIDE
    z, k = my_col // 2, my_col % 2
    outer, inner = jnp.repeat(rel, SIDE), jnp.tile(rel, SIDE)

    def describe(dy, dx):
        py, px = (y + dy) % SIDE, (x + dx) % SIDE
        strip_k = (px >> 1) ^ k
        panel = (px & 1) ^ strip_k
        return panel, ((py + z) % SIDE) * 2 + strip_k

    first, second = describe(outer, inner), describe(inner, outer)
    return jnp.stack([first[0], first[1], second[0], second[1]])


def split(value):
    high = value.astype(BF16)
    return high, (value - high.astype(F32)).astype(BF16)


def dot3(a_high, a_low, b_high, b_low, dims):
    dot = functools.partial(
        lax.dot_general, dimension_numbers=(dims, ((), ())), preferred_element_type=F32
    )
    return dot(a_high, b_high) + (dot(a_high, b_low) + dot(a_low, b_high))


def piece_blocks(pieces):
    found, position = [], 0
    for ref in pieces:
        for block in range(ref.shape[0]):
            found.append((ref, block, position))
            position += 1
    return found


def pair_kernel(order, panel_order, *refs):
    first, second, panels = refs[:5], refs[5:10], refs[10:15]
    coulomb, keep, send = refs[15:18]
    column, panel, p_high, p_low, total, column_sem, panel_sem = refs[18:]
    rows = first[0].shape[1]
    lanes = first[0].shape[2]
    panel_copies = []
    for ref, block, position in piece_blocks(panels):
        lane = pl.multiple_of(panel_order[position] * lanes, lanes)
        panel_copies.append(
            pltpu.make_async_copy(ref.at[block], panel.at[:, pl.ds(lane, lanes)], panel_sem.at[position])
        )
        panel_copies[-1].start()
    for which, pieces in enumerate((first, second)):
        for ref, block, position in piece_blocks(pieces):
            part = order[2 * which, position] * 2 + which
            strip = order[2 * which + 1, position]
            row = pl.multiple_of(part * rows, rows)
            lane = pl.multiple_of(strip * lanes, lanes)
            pltpu.make_async_copy(
                ref.at[block],
                column.at[pl.ds(row, rows), pl.ds(lane, lanes)],
                column_sem.at[part * 8 + strip],
            ).start()
    for copy in panel_copies:
        copy.wait()
    p_high[...], p_low[...] = split(panel[...])
    total[...] = jnp.zeros_like(total)

    @pl.loop(0, 4)
    def _(step):
        part = lax.rem(step, 2) * 2 + step // 2
        here = pl.ds(pl.multiple_of(part * rows, rows), rows)
        for strip in range(8):
            pltpu.make_async_copy(
                first[0].at[0], column.at[here, pl.ds(strip * lanes, lanes)], column_sem.at[part * 8 + strip]
            ).wait()
        high, low = split(column[here, :])
        pair = dot3(p_high[...], p_low[...], high, low, ((1,), (1,)))
        t_high, t_low = split(coulomb[:, here] * pair)
        total[...] += dot3(t_high, t_low, high, low, ((1,), (0,)))

    core, height = panel_order[8], panel_order[9]
    count = keep.shape[1]
    for turn in range(SIDE):
        strip = lax.rem(height + turn, SIDE) * 2
        keep[turn] = total[pl.ds(pl.multiple_of((strip + core) * count, count), count), :]
        send[turn] = total[pl.ds(pl.multiple_of((strip + 1 - core) * count, count), count), :]


def pair_weights(order, panel_order, column_pieces, panel_pieces, coulomb):
    rows, width = coulomb.shape
    bands = 8 * 128
    anywhere = pl.BlockSpec(memory_space=pl.ANY)
    scalars = pl.BlockSpec(memory_space=pltpu.SMEM)
    vmem = pl.BlockSpec(memory_space=pltpu.VMEM)
    out = jax.ShapeDtypeStruct((SIDE, rows // 8, bands), F32)
    return pl.pallas_call(
        pair_kernel,
        out_shape=(out, out),
        in_specs=[scalars, scalars] + [anywhere] * 15 + [vmem],
        out_specs=(vmem, vmem),
        scratch_shapes=[
            pltpu.VMEM((width, bands), F32),
            pltpu.VMEM((rows, bands), F32),
            pltpu.VMEM((rows, bands), BF16),
            pltpu.VMEM((rows, bands), BF16),
            pltpu.VMEM((rows, bands), F32),
            pltpu.SemaphoreType.DMA((32,)),
            pltpu.SemaphoreType.DMA((8,)),
        ],
        compiler_params=pltpu.CompilerParams(vmem_limit_bytes=26 << 20),
        cost_estimate=pl.CostEstimate(flops=12 * rows * width * bands, bytes_accessed=12 << 20, transcendentals=0),
        name="pair_weights",
    )(order, panel_order, *column_pieces, *panel_pieces, coulomb)


def term_kernel(groups, gathered, where, *refs):
    refs = list(refs)
    if gathered:
        order, first, second = refs[0], refs[1:6], refs[6:11]
        refs = refs[11:]
        outs, (high, low, whole, sem) = refs[1:-4], refs[-4:]

        @pl.when(pl.program_id(0) == 0)
        def _():
            rows = first[0].shape[1]
            copies = []
            for which, pieces in enumerate((first, second)):
                for ref, block, position in piece_blocks(pieces):
                    strip = order[2 * which, position] * 8 + order[2 * which + 1, position]
                    row = pl.multiple_of((strip * 2 + which) * rows, rows)
                    copies.append(
                        pltpu.make_async_copy(
                            ref.at[block], whole.at[pl.ds(row, rows), :], sem.at[which * 16 + position]
                        )
                    )
            for copy in copies:
                copy.start()
            for copy in copies:
                copy.wait()
            high[...], low[...] = split(whole[...])
    else:
        weights, outs = refs[1 : 1 + 2 * groups], refs[2 + 2 * groups :]
    f_high, f_low = split(refs[0][...])
    even = where[SIDE] == 0
    half = outs[0].shape[1]
    bands = 2 * half
    for group in range(groups):
        if gathered:
            here = pl.ds(pl.multiple_of(where[group] * bands, bands), bands)
            w_high, w_low = high[:, here], low[:, here]
        else:
            w_high, w_low = weights[2 * group][...], weights[2 * group + 1][...]
        product = dot3(f_high, f_low, w_high, w_low, ((1,), (0,)))
        lower, upper = product[:, :half], product[:, half:]
        outs[2 * group][...] = jnp.where(even, lower, upper)
        outs[2 * group + 1][...] = jnp.where(even, upper, lower)


def term(groups, where, fitting, weights=None, after=None, order=None, pieces=None):
    rows, points = fitting.shape
    bands = 8 * 128
    tile = 512
    gathered = pieces is not None
    halves = 2 * groups
    anywhere = pl.BlockSpec(memory_space=pltpu.HBM)
    streamed = pl.BlockSpec((tile, points), lambda i, where: (i, 0))
    resident = pl.BlockSpec((points, bands), lambda i, where: (0, 0), pipeline_mode=pl.Buffered(1))
    half = pl.BlockSpec((tile, bands // 8), lambda i, where: (i, 0))
    out = [jax.ShapeDtypeStruct((rows, bands // 8), F32)] * halves
    out_specs = [half] * halves
    scratch = []
    if gathered:
        in_specs = [pl.BlockSpec(memory_space=pltpu.SMEM)] + [anywhere] * 10 + [streamed]
        operands = (order, *pieces, fitting)
        out += [jax.ShapeDtypeStruct((points, bands), BF16)] * 2
        out_specs += [resident] * 2
        scratch = [pltpu.VMEM((points, bands), F32), pltpu.SemaphoreType.DMA((32,))]
    else:
        in_specs, operands = [streamed], [fitting]
        for group in range(groups):
            chosen = pl.BlockSpec((points, bands // SIDE), lambda i, where, group=group: (0, where[group]))
            in_specs += [chosen, chosen]
            operands += weights
        in_specs.append(anywhere)
        operands.append(after)
    return pl.pallas_call(
        functools.partial(term_kernel, groups, gathered),
        out_shape=out,
        grid_spec=pltpu.PrefetchScalarGridSpec(
            num_scalar_prefetch=1,
            grid=(rows // tile,),
            in_specs=in_specs,
            out_specs=out_specs,
            scratch_shapes=scratch,
        ),
        cost_estimate=pl.CostEstimate(
            flops=6 * groups * rows * points * bands // SIDE, bytes_accessed=11 << 20, transcendentals=0
        ),
        name="term",
    )(where, *operands)


def picked_strip(orbitals, point_index, my_row):
    row_count = SIDE * SIDE
    slab_rows, lanes = orbitals.shape
    per_panel = point_index.shape[0] // row_count
    slot_count = 2 * per_panel // row_count
    owner = point_index // slab_rows
    owner_grid = owner.reshape(row_count, per_panel)
    local_grid = (point_index - owner * slab_rows).reshape(row_count, per_panel)
    spot = jnp.arange(per_panel)
    earlier = (spot[:, None] < spot[None, :]).astype(BF16)
    mine = owner_grid == my_row
    rank = jnp.dot(mine.astype(BF16), earlier, preferred_element_type=F32).astype(jnp.int32)
    chosen = mine[:, :, None] & (rank[:, :, None] == jnp.arange(slot_count)[None, None, :])
    source_row = jnp.sum(jnp.where(chosen, local_grid[:, :, None], 0), axis=1)
    outgoing = orbitals[source_row.reshape(-1)].reshape(row_count, slot_count, lanes)
    received = lax.all_to_all(outgoing, "row", split_axis=0, concat_axis=0, tiled=True)
    owner_mine = lax.dynamic_slice_in_dim(owner_grid, my_row, 1, 0)[0]
    matches = owner_mine[None, :] == jnp.arange(row_count)[:, None]
    ranks = jnp.dot(matches.astype(BF16), earlier, preferred_element_type=F32).astype(jnp.int32)
    slot_mine = jnp.sum(jnp.where(matches, ranks, 0), axis=0)
    return received.reshape(row_count * slot_count, lanes)[owner_mine * slot_count + slot_mine]


def exchange(orbitals, point_index, coulomb, fitting):
    my_row = lax.axis_index("row")
    my_col = lax.axis_index("col")
    height, core = my_col // 2, my_col % 2
    order = plane_order(my_row, my_col)
    strip = picked_strip(orbitals, point_index, my_row)

    column_pieces = gather_plane(to_plane(strip, 0))
    both = jnp.stack([strip, swap_cores(strip)])
    before, after = move(both, "z", 1), move(both, "z", -1)
    panel_pieces = (both, before, after, move(before[:1], "z", 1), move(after[1:], "z", -1))
    place = jnp.array(REL, jnp.int32).repeat(2)
    cores = jnp.tile(jnp.array([0, 1], jnp.int32), SIDE)
    panel_order = jnp.concatenate(
        [((height + place) % SIDE) * 2 + (core ^ cores), jnp.stack([core, height])]
    ).astype(jnp.int32)
    keep, send = pair_weights(order, panel_order, column_pieces, panel_pieces, coulomb)

    summed = keep + swap_cores(send)
    parts = [to_plane(summed[turn], turn) for turn in range(SIDE)]
    w_strip = (parts[0] + parts[1]) + (parts[2] + parts[3])
    pieces = gather_plane(w_strip)

    def targets(*steps):
        chips = [(height + step) % SIDE for step in steps] + [height] * (SIDE - len(steps))
        return jnp.stack(chips + [core]).astype(jnp.int32)

    half = fitting.shape[0] // 2
    mine, other, *weights = term(1, targets(2), fitting, order=order, pieces=pieces)
    far = mine + swap_cores(other)
    far_up = move(far[:half], "z", 1)
    far_down = move(far[half:], "z", -1)
    chips, tag = targets(1, -1), far[:8]
    mine, other, mine_down, other_down = term(2, chips, fitting, weights, tag)
    up = mine + swap_cores(other)
    down = mine_down + swap_cores(other_down)
    up_high = move(up[half:], "z", 1)
    down_low = move(down[:half], "z", -1)
    up_low = move(up[:half] + far_up, "z", 1)
    down_high = move(down[half:] + far_down, "z", -1)
    chips, tag = targets(0), up[:8] + down[:8]
    mine, other = term(1, chips, fitting, weights, tag)
    own = mine + swap_cores(other)
    low = own[:half] + (up_low + down_low)
    high = own[half:] + (up_high + down_high)
    return -jnp.concatenate([low, high], axis=0)


def solution(mesh):
    in_specs = (P("row", "col"), P(), P("row", "col"), P("row", "col"))
    out_specs = P("row", "col")
    return jax.shard_map(exchange, mesh=mesh, in_specs=in_specs, out_specs=out_specs, check_vma=False)
```

time: 456 us -> 259 us (0.57)
  waiting for transfers between devices: 284 us -> 81.6 us
  starting transfers between devices: 13 us -> 94.4 us
  blocking collectives: 53.9 us -> 0 us
  matrix products: 49.4 us -> 0.38 us
  Pallas kernels: 0 us -> 47.6 us
  between operations: 13.3 us -> 0.64 us
  other arithmetic: 21.4 us -> 9.97 us
    all_gather x3 -> x0, waiting for transfers between devices: 135 us -> none  [the longest x1 52.7 us: per_device(): weight_all = lax.all_gather(weight_strip, 'row', axis=0, tiled=True)]
    ppermute x0 -> x53, starting transfers between devices: none -> 86.7 us  [the longest x42 47.1 us: move(): return lax.ppermute(value, name, pairs)]
    ppermute x0 -> x53, waiting for transfers between devices: none -> 71.4 us  [the longest x42 56.9 us: move(): return lax.ppermute(value, name, pairs)]
    psum x1 -> x0, waiting for transfers between devices: 62.2 us -> none  [per_device(): summed = lax.psum(partial_value, 'col')]
    all_to_all x1 -> x0, blocking collectives: 53.9 us -> none  [per_device(): lax.all_to_all(weight_all, 'col', split_axis=0, concat_axis=1, tiled=True)]
    reduce_scatter x1 -> x0, waiting for transfers between devices: 50.2 us -> none  [per_device(): return lax.psum_scatter(term, 'col', scatter_dimension=1, tiled=True)]
    dot_general x3 -> x2, matrix products: 49.4 us -> 0.38 us  [the longest x1 0.2 us: picked_strip(): jnp.dot(matches.astype(BF16), earlier, preferred_element_type=F32)]
    pallas_call x0 -> x4, Pallas kernels: none -> 47.6 us  [the longest x3 31.3 us: term(): pl.pallas_call(functools.partial(term_kernel, groups, gathered), out_shap...]
  transfers between devices with their start and end apart: 7 -> 54, of which waited for: 7 -> 22; matrix products, arithmetic and copies ran while one was open for 1% -> 8% of each run, Pallas kernels for 0% -> 3%
where the time goes in v1:
time: 259 us; the launch traced here: 257 us
  starting transfers between devices  94.4 us (36%)
  waiting for transfers between devices  81.6 us (32%)
  Pallas kernels  47.6 us (18%)
  local copies, waits for them, and re-layouts  22.3 us (9%)
  other arithmetic  9.97 us (4%)
    ppermute x42, waiting for transfers between devices, move(): return lax.ppermute(value, name, pairs)  56.9 us
    ppermute x42, starting transfers between devices, move(): return lax.ppermute(value, name, pairs)  47.1 us
    pallas_call x3, Pallas kernels, term(): pl.pallas_call(functools.partial(term_kernel, groups, gathered), out_shap...  31.3 us
    ppermute x5, starting transfers between devices, to_plane(): return lax.ppermute(value, ('row', 'col'), scatter_pairs(turn))  21.2 us
    ppermute x6, starting transfers between devices, swap_cores(): return lax.ppermute(value, 'col', [(c, c ^ 1) for c in range(2 * SIDE)])  18.4 us
    pallas_call x1, Pallas kernels, pair_weights(): pl.pallas_call(pair_kernel, out_shape=(out, out), in_specs=[scalars, scal...  16.3 us
    ppermute x5, waiting for transfers between devices, to_plane(): return lax.ppermute(value, ('row', 'col'), scatter_pairs(turn))  10.4 us
    all_to_all x1, waiting for transfers between devices, picked_strip(): lax.all_to_all(outgoing, 'row', split_axis=0, concat_axis=0, tiled=True)  10.2 us
  transfers between devices with their start and end apart: 54, of which 22 were waited for; matrix products, arithmetic and copies ran while one was open for 8% of the time, Pallas kernels for 3%

profile of v1, /device:TPU:1, one launch (start us, length us, event | category | flops | bytes accessed | tf_op | source)
XLA Modules:
  0.0 256.9 jit_solution(17158895227563527320)
XLA Ops:
  1.8 4.0 %gather_fusion = f32[1024,128]{1,0:T(8,128)} fusion(f32[2048,128]{1,0:T(8,128)S(1)} %copy-done, s32[1024]{0:T(1024)S(1)} %broadcast_clamp_fusion), kind=kCustom, calls=%fused_computation | custom fusion | bytes 1052672 | tf_op jit(solution)/shard_map/gather | solution.py:293
  5.8 7.7 %all-to-all-start = ((f32[16,64,128]{2,1,0:T(8,128)}), f32[16,64,128]{2,1,0:T(8,128)S(1)}, u32[]{:S(2)}, u32[]{:S(2)}) async-start(f32[16,64,128]{2,1,0:T(8,128)} %bitcast.5), calls=%async_computation | async-start | bytes 1048576 | tf_op jit(solution)/shard_map/all_to_all | solution.py:294
  13.8 10.2 %all-to-all-done = f32[16,64,128]{2,1,0:T(8,128)S(1)} async-done(((f32[16,64,128]{2,1,0:T(8,128)}), f32[16,64,128]{2,1,0:T(8,128)S(1)}, u32[]{:S(2)}, u32[]{:S(2)}) %all-to-all-start) | async-done | bytes 524320 | tf_op jit(solution)/shard_map/all_to_all | solution.py:294
  23.9 1.0 gather_fusion.1
  25.0 4.1 %collective-permute-start = (f32[512,128]{1,0:T(8,128)S(1)}, f32[512,128]{1,0:T(8,128)S(1)}, u32[]{:S(2)}, u32[]{:S(2)}) collective-permute-start(f32[512,128]{1,0:T(8,128)S(1)} %gather_fusion.1), channel_id=1, source_target_pairs={{0,0},{1,24},{2,32},{3,56},{4,64},{5,88},{6,96},{7,120},{8,8},{9,1... | collective-permute-start | bytes 786440 | tf_op jit(solution)/shard_map/ppermute | solution.py:56
  29.3 4.0 %collective-permute-done = f32[512,128]{1,0:T(8,128)S(1)} collective-permute-done((f32[512,128]{1,0:T(8,128)S(1)}, f32[512,128]{1,0:T(8,128)S(1)}, u32[]{:S(2)}, u32[]{:S(2)}) %collective-permute-start) | collective-permute-done | bytes 262176 | tf_op jit(solution)/shard_map/ppermute | solution.py:56
  34.0 5.2 %collective-permute-start.10 = (f32[256,128]{1,0:T(8,128)}, f32[256,128]{1,0:T(8,128)S(1)}, u32[]{:S(2)}, u32[]{:S(2)}) collective-permute-start(f32[256,128]{1,0:T(8,128)} %get-tuple-element.49), channel_id=1, source_target_pairs={{0,96},{8,104},{16,112},{24,120},{32,0},{40,8},{48,16},{56,24},{64... | collective-permute-start | bytes 393224 | tf_op jit(solution)/shard_map/ppermute | solution.py:34
  39.9 2.9 %collective-permute-start.19 = (f32[2,512,128]{2,1,0:T(8,128)S(1)}, f32[2,512,128]{2,1,0:T(8,128)S(1)}, u32[]{:S(2)}, u32[]{:S(2)}) collective-permute-start(f32[2,512,128]{2,1,0:T(8,128)S(1)} %pad_maximum_fusion.refs_10_), channel_id=1, source_target_pairs={{0,6},{1,7},{2,0},{3,1},{4,2},{5,3},{6,4},{7,5},{8,14},{9,15},{10,... | collective-permute-start | bytes 1572872 | tf_op jit(solution)/shard_map/ppermute | solution.py:34
  42.9 3.4 %collective-permute-start.2 = (f32[256,128]{1,0:T(8,128)S(1)}, f32[256,128]{1,0:T(8,128)S(1)}, u32[]{:S(2)}, u32[]{:S(2)}) collective-permute-start(f32[256,128]{1,0:T(8,128)S(1)} %get-tuple-element.52), channel_id=1, source_target_pairs={{0,24},{8,0},{16,8},{24,16},{32,56},{40,32},{48,40},{56,48},{64,88... | collective-permute-start | bytes 393224 | tf_op jit(solution)/shard_map/ppermute | solution.py:34
  46.3 3.2 %collective-permute-start.12 = (f32[128,128]{1,0:T(8,128)S(1)}, f32[128,128]{1,0:T(8,128)S(1)}, u32[]{:S(2)}, u32[]{:S(2)}) collective-permute-start(f32[128,128]{1,0:T(8,128)S(1)} %slice.159), channel_id=1, source_target_pairs={{0,96},{8,104},{16,112},{24,120},{32,0},{40,8},{48,16},{56,24},{64... | collective-permute-start | bytes 196616 | tf_op jit(solution)/shard_map/ppermute | solution.py:34
  51.0 4.6 %collective-permute-done.3 = f32[128,128]{1,0:T(8,128)S(1)} collective-permute-done((f32[128,128]{1,0:T(8,128)S(1)}, f32[128,128]{1,0:T(8,128)S(1)}, u32[]{:S(2)}, u32[]{:S(2)}) %collective-permute-start.3) | collective-permute-done | bytes 65568 | tf_op jit(solution)/shard_map/ppermute | solution.py:34
  56.0 3.0 %collective-permute-done.4 = f32[128,128]{1,0:T(8,128)S(1)} collective-permute-done((f32[128,128]{1,0:T(8,128)S(1)}, f32[128,128]{1,0:T(8,128)S(1)}, u32[]{:S(2)}, u32[]{:S(2)}) %collective-permute-start.4) | collective-permute-done | bytes 65568 | tf_op jit(solution)/shard_map/ppermute | solution.py:34
  59.8 2.7 %collective-permute-start.6 = (f32[4,256,128]{2,1,0:T(8,128)}, f32[4,256,128]{2,1,0:T(8,128)S(1)}, u32[]{:S(2)}, u32[]{:S(2)}) collective-permute-start(f32[4,256,128]{2,1,0:T(8,128)} %bitcast.31), channel_id=1, source_target_pairs={{0,96},{8,104},{16,112},{24,120},{32,0},{40,8},{48,16},{56,24},{64... | collective-permute-start | bytes 1572872 | tf_op jit(solution)/shard_map/ppermute | solution.py:34
  63.7 0.9 collective-permute-start.14
  67.2 1.7 collective-permute-done.6.refs_2_
  68.9 3.1 %collective-permute-done.5.refs_1_ = f32[4,256,128]{2,1,0:T(8,128)} collective-permute-done((f32[4,256,128]{2,1,0:T(8,128)}, f32[4,256,128]{2,1,0:T(8,128)}, u32[]{:S(2)}, u32[]{:S(2)}) %collective-permute-start.5) | collective-permute-done | bytes 524320 | tf_op jit(solution)/shard_map/ppermute | solution.py:34
  72.0 1.0 slice.155
  73.0 1.5 collective-permute-start.7
  74.5 1.0 slice.161
  75.5 1.0 collective-permute-start.16
  76.5 1.0 slice.160
  78.4 2.6 collective-permute-done.7.refs_3_
  81.0 3.2 %collective-permute-done.15.refs_8_ = f32[2,256,128]{2,1,0:T(8,128)S(1)} collective-permute-done((f32[2,256,128]{2,1,0:T(8,128)S(1)}, f32[2,256,128]{2,1,0:T(8,128)S(1)}, u32[]{:S(2)}, u32[]{:S(2)}) %collective-permute-start.15) | collective-permute-done | bytes 262176 | tf_op jit(solution)/shard_map/ppermute | solution.py:34
  84.1 1.6 copy-done.5
  85.7 16.3 %pair_weights.1 = (f32[4,64,1024]{2,1,0:T(8,128)S(1)}, f32[4,64,1024]{2,1,0:T(8,128)S(1)}) custom-call(s32[4,16]{1,0:T(4,128)S(1)} %pad_add_fusion.order.refs_0_, s32[10]{0:T(128)S(1)} %pad_add_fusion.1.panel_order, f32[4,256,128]{2,1,0:T(8,128)S(1)} %bitcast.33, f32[4,256,128]{2,1,0:T(8,128)} %collective-permute-done.5.refs_1_, ...), custom_call_target="tpu_custom_call" | custom-call | flops 6442450944 | bytes 12582912 | tf_op jit(solution)/shard_map/pair_weights/pallas_call | solution.py:172
  102.0 11.6 %collective-permute-start.22 = (f32[4,64,1024]{2,1,0:T(8,128)S(1)}, f32[4,64,1024]{2,1,0:T(8,128)S(1)}, u32[]{:S(2)}, u32[]{:S(2)}) collective-permute-start(f32[4,64,1024]{2,1,0:T(8,128)S(1)} %get-tuple-element.18), channel_id=1, source_target_pairs={{0,1},{1,0},{2,3},{3,2},{4,5},{5,4},{6,7},{7,6},{8,9},{9,8},{10,11... | collective-permute-start | bytes 3145736 | tf_op jit(solution)/shard_map/ppermute | solution.py:38
  113.6 2.3 collective-permute-done.22
  116.1 1.9 collective-permute-start.24
  118.0 4.2 %collective-permute-start.26 = (f32[64,1024]{1,0:T(8,128)S(1)}, f32[64,1024]{1,0:T(8,128)S(1)}, u32[]{:S(2)}, u32[]{:S(2)}) collective-permute-start(f32[64,1024]{1,0:T(8,128)S(1)} %get-tuple-element.42), channel_id=1, source_target_pairs={{0,96},{1,120},{2,0},{3,24},{4,32},{5,56},{6,64},{7,88},{8,104},{9... | collective-permute-start | bytes 786440 | tf_op jit(solution)/shard_map/ppermute | solution.py:56
  122.2 9.1 %collective-permute-start.25 = (f32[64,1024]{1,0:T(8,128)S(1)}, f32[64,1024]{1,0:T(8,128)S(1)}, u32[]{:S(2)}, u32[]{:S(2)}) collective-permute-start(f32[64,1024]{1,0:T(8,128)S(1)} %get-tuple-element.43), channel_id=1, source_target_pairs={{0,64},{1,88},{2,96},{3,120},{4,0},{5,24},{6,32},{7,56},{8,72},{9,... | collective-permute-start | bytes 786440 | tf_op jit(solution)/shard_map/ppermute | solution.py:56
  131.3 1.9 collective-permute-start.23
  133.2 2.1 collective-permute-done.25
  135.3 4.3 %collective-permute-done.23 = f32[64,1024]{1,0:T(8,128)S(1)} collective-permute-done((f32[64,1024]{1,0:T(8,128)S(1)}, f32[64,1024]{1,0:T(8,128)S(1)}, u32[]{:S(2)}, u32[]{:S(2)}) %collective-permute-start.23) | collective-permute-done | bytes 262176 | tf_op jit(solution)/shard_map/ppermute | solution.py:56
  139.7 2.1 collective-permute-start.36
  141.8 1.7 collective-permute-start.28
  143.5 1.2 collective-permute-done.36
  144.7 3.4 %collective-permute-start.38 = (f32[16,1024]{1,0:T(8,128)S(1)}, f32[16,1024]{1,0:T(8,128)S(1)}, u32[]{:S(2)}, u32[]{:S(2)}) collective-permute-start(f32[16,1024]{1,0:T(8,128)S(1)} %slice.175), channel_id=1, source_target_pairs={{0,96},{8,104},{16,112},{24,120},{32,0},{40,8},{48,16},{56,24},{64... | collective-permute-start | bytes 196616 | tf_op jit(solution)/shard_map/ppermute | solution.py:34
  148.6 1.4 collective-permute-start.30
  150.3 4.4 %collective-permute-done.29 = f32[16,1024]{1,0:T(8,128)S(1)} collective-permute-done((f32[16,1024]{1,0:T(8,128)S(1)}, f32[16,1024]{1,0:T(8,128)S(1)}, u32[]{:S(2)}, u32[]{:S(2)}) %collective-permute-start.29) | collective-permute-done | bytes 65568 | tf_op jit(solution)/shard_map/ppermute | solution.py:34
  154.8 2.4 collective-permute-start.32
  157.4 1.5 collective-permute-start.39
  158.8 6.8 %collective-permute-done.32.refs_3_ = f32[4,32,1024]{2,1,0:T(8,128)S(1)} collective-permute-done((f32[4,32,1024]{2,1,0:T(8,128)S(1)}, f32[4,32,1024]{2,1,0:T(8,128)S(1)}, u32[]{:S(2)}, u32[]{:S(2)}) %collective-permute-start.32) | collective-permute-done | bytes 524320 | tf_op jit(solution)/shard_map/ppermute | solution.py:34
  166.4 3.3 %collective-permute-start.34 = (f32[2,32,1024]{2,1,0:T(8,128)}, f32[2,32,1024]{2,1,0:T(8,128)S(1)}, u32[]{:S(2)}, u32[]{:S(2)}) collective-permute-start(f32[2,32,1024]{2,1,0:T(8,128)} %slice.172), channel_id=1, source_target_pairs={{0,96},{8,104},{16,112},{24,120},{32,0},{40,8},{48,16},{56,24},{64... | collective-permute-start | bytes 786440 | tf_op jit(solution)/shard_map/ppermute | solution.py:34
  172.2 1.3 collective-permute-start.41
  174.2 3.0 %collective-permute-done.33.refs_4_ = f32[2,32,1024]{2,1,0:T(8,128)} collective-permute-done((f32[2,32,1024]{2,1,0:T(8,128)}, f32[2,32,1024]{2,1,0:T(8,128)}, u32[]{:S(2)}, u32[]{:S(2)}) %collective-permute-start.33) | collective-permute-done | bytes 262176 | tf_op jit(solution)/shard_map/ppermute | solution.py:34
  177.2 1.8 collective-permute-done.41.refs_9_
  179.0 11.8 %term.3 = (f32[2048,128]{1,0:T(8,128)}, f32[2048,128]{1,0:T(8,128)}, bf16[1024,1024]{1,0:T(8,128)(2,1)}, bf16[1024,1024]{1,0:T(8,128)(2,1)}) custom-call(s32[5]{0:T(128)} %stack.59.where, s32[4,16]{1,0:T(4,128)} %copy-done.4, f32[4,32,1024]{2,1,0:T(8,128)} %bitcast.41, f32[4,32,1024]{2,1,0:T(8,128)} %copy-done.7, f32[4,32,1024]{2,1,0:T(8,128)} %copy-done.6, ...), custom_call_target="tpu_custom_call" | custom-call | flops 3221225472 | bytes 11534336 | tf_op jit(solution)/shard_map/term/pallas_call | solution.py:262
  190.8 5.4 %collective-permute-start.43 = (f32[2048,128]{1,0:T(8,128)}, f32[2048,128]{1,0:T(8,128)S(1)}, u32[]{:S(2)}, u32[]{:S(2)}) collective-permute-start(f32[2048,128]{1,0:T(8,128)} %get-tuple-element.22), channel_id=1, source_target_pairs={{0,1},{1,0},{2,3},{3,2},{4,5},{5,4},{6,7},{7,6},{8,9},{9,8},{10,11... | collective-permute-start | bytes 3145736 | tf_op jit(solution)/shard_map/ppermute | solution.py:38
  196.8 1.9 collective-permute-done.43
  198.7 1.3 add.366
  200.6 11.3 %term.4 = (f32[2048,128]{1,0:T(8,128)}, f32[2048,128]{1,0:T(8,128)}, f32[2048,128]{1,0:T(8,128)}, f32[2048,128]{1,0:T(8,128)}) custom-call(s32[5]{0:T(128)} %stack.66.where, f32[2048,1024]{1,0:T(8,128)} %refs_0_.3, bf16[1024,1024]{1,0:T(8,128)(2,1)} %get-tuple-element.19.refs_1_.refs_3_, bf16[1024,1024]{1,0:T(8,128)(2,1)} %get-tuple-element.20.refs_2_.refs_4_, ...), custom_call_target="tpu_custom_call" | custom-call | flops 6442450944 | bytes 11534336 | tf_op jit(solution)/shard_map/term/pallas_call | solution.py:262
  213.0 1.1 fusion.22
  214.1 2.3 collective-permute-start.47
  216.9 1.3 add.368
  218.8 8.3 %term.5 = (f32[2048,128]{1,0:T(8,128)}, f32[2048,128]{1,0:T(8,128)}) custom-call(s32[5]{0:T(128)} %stack.57.where, f32[2048,1024]{1,0:T(8,128)} %refs_0_.3, bf16[1024,1024]{1,0:T(8,128)(2,1)} %get-tuple-element.19.refs_1_.refs_3_, bf16[1024,1024]{1,0:T(8,128)(2,1)} %get-tuple-element.20.refs_2_.refs_4_, f32[8,128]{1,0:T(8,128)} %slice_add_fusion.4.refs_3_), custom_call_target="tpu_custom_call" | custom-call | flops 3221225472 | bytes 11534336 | tf_op jit(solution)/shard_map/term/pallas_call | solution.py:262
  227.1 0.9 collective-permute-start.46
  228.7 1.1 slice_add_fusion.2
  229.9 1.2 collective-permute-start.48
  231.3 1.1 fusion.21
  232.4 2.5 collective-permute-start.49
  235.4 8.0 %collective-permute-done.48 = f32[1024,128]{1,0:T(8,128)S(1)} collective-permute-done((f32[1024,128]{1,0:T(8,128)S(1)}, f32[1024,128]{1,0:T(8,128)S(1)}, u32[]{:S(2)}, u32[]{:S(2)}) %collective-permute-start.48) | collective-permute-done | bytes 524320 | tf_op jit(solution)/shard_map/ppermute | solution.py:34
  243.4 11.2 %collective-permute-done.50 = f32[1024,128]{1,0:T(8,128)S(1)} collective-permute-done((f32[1024,128]{1,0:T(8,128)S(1)}, f32[1024,128]{1,0:T(8,128)S(1)}, u32[]{:S(2)}, u32[]{:S(2)}) %collective-permute-start.50) | collective-permute-done | bytes 524320 | tf_op jit(solution)/shard_map/ppermute | solution.py:34
  254.6 1.1 collective-permute-done.52
  255.9 1.0 maximum_negate_fusion
  (171 shorter events, 21.2 us)
Async XLA Ops:
  5.8 23.3 %copy-start.16 = (s32[4]{0:T(128)S(1)}, s32[4]{0:T(128)}, u32[]{:S(2)}) copy-start(s32[4]{0:T(128)} %constant.146.clone) | copy-start | bytes 52
  5.8 18.1 %all-to-all-start = ((f32[16,64,128]{2,1,0:T(8,128)}), f32[16,64,128]{2,1,0:T(8,128)S(1)}, u32[]{:S(2)}, u32[]{:S(2)}) async-start(f32[16,64,128]{2,1,0:T(8,128)} %bitcast.5), calls=%async_computation | async-start | bytes 1048576 | tf_op jit(solution)/shard_map/all_to_all | solution.py:294
  25.0 8.3 %collective-permute-start = (f32[512,128]{1,0:T(8,128)S(1)}, f32[512,128]{1,0:T(8,128)S(1)}, u32[]{:S(2)}, u32[]{:S(2)}) collective-permute-start(f32[512,128]{1,0:T(8,128)S(1)} %gather_fusion.1), channel_id=1, source_target_pairs={{0,0},{1,24},{2,32},{3,56},{4,64},{5,88},{6,96},{7,120},{8,8},{9,1... | collective-permute-start | bytes 786440 | tf_op jit(solution)/shard_map/ppermute | solution.py:56
  29.3 10.6 %collective-permute-start.17 = (f32[512,128]{1,0:T(8,128)S(1)}, f32[512,128]{1,0:T(8,128)S(1)}, u32[]{:S(2)}, u32[]{:S(2)}) collective-permute-start(f32[512,128]{1,0:T(8,128)S(1)} %gather_fusion.1), channel_id=1, source_target_pairs={{0,1},{1,0},{2,3},{3,2},{4,5},{5,4},{6,7},{7,6},{8,9},{9,8},{10,11... | collective-permute-start | bytes 786440 | tf_op jit(solution)/shard_map/ppermute | solution.py:38
  34.0 8.8 %collective-permute-start.10 = (f32[256,128]{1,0:T(8,128)}, f32[256,128]{1,0:T(8,128)S(1)}, u32[]{:S(2)}, u32[]{:S(2)}) collective-permute-start(f32[256,128]{1,0:T(8,128)} %get-tuple-element.49), channel_id=1, source_target_pairs={{0,96},{8,104},{16,112},{24,120},{32,0},{40,8},{48,16},{56,24},{64... | collective-permute-start | bytes 393224 | tf_op jit(solution)/shard_map/ppermute | solution.py:34
  39.2 7.0 %collective-permute-start.9 = (f32[256,128]{1,0:T(8,128)}, f32[256,128]{1,0:T(8,128)S(1)}, u32[]{:S(2)}, u32[]{:S(2)}) collective-permute-start(f32[256,128]{1,0:T(8,128)} %get-tuple-element.49), channel_id=1, source_target_pairs={{0,32},{8,40},{16,48},{24,56},{32,64},{40,72},{48,80},{56,88},{64,... | collective-permute-start | bytes 393224 | tf_op jit(solution)/shard_map/ppermute | solution.py:34
  39.9 10.3 %collective-permute-start.1 = (f32[256,128]{1,0:T(8,128)S(1)}, f32[256,128]{1,0:T(8,128)S(1)}, u32[]{:S(2)}, u32[]{:S(2)}) collective-permute-start(f32[256,128]{1,0:T(8,128)S(1)} %get-tuple-element.52), channel_id=1, source_target_pairs={{0,8},{8,16},{16,24},{24,0},{32,40},{40,48},{48,56},{56,32},{64,72... | collective-permute-start | bytes 393224 | tf_op jit(solution)/shard_map/ppermute | solution.py:34
  39.9 24.7 %collective-permute-start.19 = (f32[2,512,128]{2,1,0:T(8,128)S(1)}, f32[2,512,128]{2,1,0:T(8,128)S(1)}, u32[]{:S(2)}, u32[]{:S(2)}) collective-permute-start(f32[2,512,128]{2,1,0:T(8,128)S(1)} %pad_maximum_fusion.refs_10_), channel_id=1, source_target_pairs={{0,6},{1,7},{2,0},{3,1},{4,2},{5,3},{6,4},{7,5},{8,14},{9,15},{10,... | collective-permute-start | bytes 1572872 | tf_op jit(solution)/shard_map/ppermute | solution.py:34
  42.9 23.1 %collective-permute-start.18 = (f32[2,512,128]{2,1,0:T(8,128)S(1)}, f32[2,512,128]{2,1,0:T(8,128)S(1)}, u32[]{:S(2)}, u32[]{:S(2)}) collective-permute-start(f32[2,512,128]{2,1,0:T(8,128)S(1)} %pad_maximum_fusion.refs_10_), channel_id=1, source_target_pairs={{0,2},{1,3},{2,4},{3,5},{4,6},{5,7},{6,0},{7,1},{8,10},{9,11},{10,... | collective-permute-start | bytes 1572872 | tf_op jit(solution)/shard_map/ppermute | solution.py:34
  42.9 8.0 %collective-permute-start.2 = (f32[256,128]{1,0:T(8,128)S(1)}, f32[256,128]{1,0:T(8,128)S(1)}, u32[]{:S(2)}, u32[]{:S(2)}) collective-permute-start(f32[256,128]{1,0:T(8,128)S(1)} %get-tuple-element.52), channel_id=1, source_target_pairs={{0,24},{8,0},{16,8},{24,16},{32,56},{40,32},{48,40},{56,48},{64,88... | collective-permute-start | bytes 393224 | tf_op jit(solution)/shard_map/ppermute | solution.py:34
  46.3 16.8 %collective-permute-start.12 = (f32[128,128]{1,0:T(8,128)S(1)}, f32[128,128]{1,0:T(8,128)S(1)}, u32[]{:S(2)}, u32[]{:S(2)}) collective-permute-start(f32[128,128]{1,0:T(8,128)S(1)} %slice.159), channel_id=1, source_target_pairs={{0,96},{8,104},{16,112},{24,120},{32,0},{40,8},{48,16},{56,24},{64... | collective-permute-start | bytes 196616 | tf_op jit(solution)/shard_map/ppermute | solution.py:34
  50.1 12.3 %collective-permute-start.11 = (f32[128,128]{1,0:T(8,128)S(1)}, f32[128,128]{1,0:T(8,128)S(1)}, u32[]{:S(2)}, u32[]{:S(2)}) collective-permute-start(f32[128,128]{1,0:T(8,128)S(1)} %slice.158), channel_id=1, source_target_pairs={{0,32},{8,40},{16,48},{24,56},{32,64},{40,72},{48,80},{56,88},{64,... | collective-permute-start | bytes 196616 | tf_op jit(solution)/shard_map/ppermute | solution.py:34
  50.9 4.6 %collective-permute-start.3 = (f32[128,128]{1,0:T(8,128)S(1)}, f32[128,128]{1,0:T(8,128)S(1)}, u32[]{:S(2)}, u32[]{:S(2)}) collective-permute-start(f32[128,128]{1,0:T(8,128)S(1)} %slice.153), channel_id=1, source_target_pairs={{0,8},{8,16},{16,24},{24,0},{32,40},{40,48},{48,56},{56,32},{64,72... | collective-permute-start | bytes 196616 | tf_op jit(solution)/shard_map/ppermute | solution.py:34
  55.5 3.4 %collective-permute-start.4 = (f32[128,128]{1,0:T(8,128)S(1)}, f32[128,128]{1,0:T(8,128)S(1)}, u32[]{:S(2)}, u32[]{:S(2)}) collective-permute-start(f32[128,128]{1,0:T(8,128)S(1)} %slice.154), channel_id=1, source_target_pairs={{0,24},{8,0},{16,8},{24,16},{32,56},{40,32},{48,40},{56,48},{64,88... | collective-permute-start | bytes 196616 | tf_op jit(solution)/shard_map/ppermute | solution.py:34
  59.8 9.1 %collective-permute-start.6 = (f32[4,256,128]{2,1,0:T(8,128)}, f32[4,256,128]{2,1,0:T(8,128)S(1)}, u32[]{:S(2)}, u32[]{:S(2)}) collective-permute-start(f32[4,256,128]{2,1,0:T(8,128)} %bitcast.31), channel_id=1, source_target_pairs={{0,96},{8,104},{16,112},{24,120},{32,0},{40,8},{48,16},{56,24},{64... | collective-permute-start | bytes 1572872 | tf_op jit(solution)/shard_map/ppermute | solution.py:34
  62.4 9.6 %collective-permute-start.5 = (f32[4,256,128]{2,1,0:T(8,128)}, f32[4,256,128]{2,1,0:T(8,128)}, u32[]{:S(2)}, u32[]{:S(2)}) collective-permute-start(f32[4,256,128]{2,1,0:T(8,128)} %bitcast.32), channel_id=1, source_target_pairs={{0,32},{8,40},{16,48},{24,56},{32,64},{40,72},{48,80},{56,88},{64,... | collective-permute-start | bytes 1572872 | tf_op jit(solution)/shard_map/ppermute | solution.py:34
  63.7 9.3 %collective-permute-start.14 = (f32[4,256,128]{2,1,0:T(8,128)}, f32[4,256,128]{2,1,0:T(8,128)}, u32[]{:S(2)}, u32[]{:S(2)}) collective-permute-start(f32[4,256,128]{2,1,0:T(8,128)} %bitcast.34), channel_id=1, source_target_pairs={{0,24},{8,0},{16,8},{24,16},{32,56},{40,32},{48,40},{56,48},{64,88... | collective-permute-start | bytes 1572872 | tf_op jit(solution)/shard_map/ppermute | solution.py:34
  64.6 10.8 %collective-permute-start.13 = (f32[4,256,128]{2,1,0:T(8,128)}, f32[4,256,128]{2,1,0:T(8,128)}, u32[]{:S(2)}, u32[]{:S(2)}) collective-permute-start(f32[4,256,128]{2,1,0:T(8,128)} %bitcast.35), channel_id=1, source_target_pairs={{0,8},{8,16},{16,24},{24,0},{32,40},{40,48},{48,56},{56,32},{64,72... | collective-permute-start | bytes 1572872 | tf_op jit(solution)/shard_map/ppermute | solution.py:34
  65.9 11.5 %collective-permute-start.21 = (f32[1,512,128]{2,1,0:T(8,128)}, f32[1,512,128]{2,1,0:T(8,128)S(1)}, u32[]{:S(2)}, u32[]{:S(2)}) collective-permute-start(f32[1,512,128]{2,1,0:T(8,128)} %slice.163), channel_id=1, source_target_pairs={{0,6},{1,7},{2,0},{3,1},{4,2},{5,3},{6,4},{7,5},{8,14},{9,15},{10,... | collective-permute-start | bytes 786440 | tf_op jit(solution)/shard_map/ppermute | solution.py:34
  66.4 17.7 %copy-start.2 = (f32[1024,128]{1,0:T(8,128)S(1)}, f32[1024,128]{1,0:T(8,128)}, u32[]{:S(2)}) copy-start(f32[1024,128]{1,0:T(8,128)} %copy-done.1) | copy-start | bytes 1572868
  66.4 17.7 %copy-start.3 = (f32[1024,128]{1,0:T(8,128)S(1)}, f32[1024,128]{1,0:T(8,128)}, u32[]{:S(2)}) copy-start(f32[1024,128]{1,0:T(8,128)} %constant_dynamic-update-slice_fusion.5) | copy-start | bytes 1572868
  68.9 9.5 %collective-permute-start.20 = (f32[1,512,128]{2,1,0:T(8,128)S(1)}, f32[1,512,128]{2,1,0:T(8,128)S(1)}, u32[]{:S(2)}, u32[]{:S(2)}) collective-permute-start(f32[1,512,128]{2,1,0:T(8,128)S(1)} %slice.162), channel_id=1, source_target_pairs={{0,2},{1,3},{2,4},{3,5},{4,6},{5,7},{6,0},{7,1},{8,10},{9,11},{10,... | collective-permute-start | bytes 786440 | tf_op jit(solution)/shard_map/ppermute | solution.py:34
  72.0 6.4 %collective-permute-start.8 = (f32[2,256,128]{2,1,0:T(8,128)S(1)}, f32[2,256,128]{2,1,0:T(8,128)S(1)}, u32[]{:S(2)}, u32[]{:S(2)}) collective-permute-start(f32[2,256,128]{2,1,0:T(8,128)S(1)} %slice.156), channel_id=1, source_target_pairs={{0,96},{8,104},{16,112},{24,120},{32,0},{40,8},{48,16},{56,24},{64... | collective-permute-start | bytes 786440 | tf_op jit(solution)/shard_map/ppermute | solution.py:34
  73.0 8.0 %collective-permute-start.7 = (f32[2,256,128]{2,1,0:T(8,128)S(1)}, f32[2,256,128]{2,1,0:T(8,128)S(1)}, u32[]{:S(2)}, u32[]{:S(2)}) collective-permute-start(f32[2,256,128]{2,1,0:T(8,128)S(1)} %slice.155), channel_id=1, source_target_pairs={{0,32},{8,40},{16,48},{24,56},{32,64},{40,72},{48,80},{56,88},{64,... | collective-permute-start | bytes 786440 | tf_op jit(solution)/shard_map/ppermute | solution.py:34
  75.5 5.5 %collective-permute-start.16 = (f32[2,256,128]{2,1,0:T(8,128)S(1)}, f32[2,256,128]{2,1,0:T(8,128)S(1)}, u32[]{:S(2)}, u32[]{:S(2)}) collective-permute-start(f32[2,256,128]{2,1,0:T(8,128)S(1)} %slice.161), channel_id=1, source_target_pairs={{0,24},{8,0},{16,8},{24,16},{32,56},{40,32},{48,40},{56,48},{64,88... | collective-permute-start | bytes 786440 | tf_op jit(solution)/shard_map/ppermute | solution.py:34
  77.5 6.7 %collective-permute-start.15 = (f32[2,256,128]{2,1,0:T(8,128)S(1)}, f32[2,256,128]{2,1,0:T(8,128)S(1)}, u32[]{:S(2)}, u32[]{:S(2)}) collective-permute-start(f32[2,256,128]{2,1,0:T(8,128)S(1)} %slice.160), channel_id=1, source_target_pairs={{0,8},{8,16},{16,24},{24,0},{32,40},{40,48},{48,56},{56,32},{64,72... | collective-permute-start | bytes 786440 | tf_op jit(solution)/shard_map/ppermute | solution.py:34
  78.4 23.7 %copy-start.4 = (s32[4,16]{1,0:T(4,128)}, s32[4,16]{1,0:T(4,128)S(1)}, u32[]{:S(2)}) copy-start(s32[4,16]{1,0:T(4,128)S(1)} %pad_add_fusion.order.refs_0_) | copy-start | bytes 772
  102.0 13.8 %collective-permute-start.22 = (f32[4,64,1024]{2,1,0:T(8,128)S(1)}, f32[4,64,1024]{2,1,0:T(8,128)S(1)}, u32[]{:S(2)}, u32[]{:S(2)}) collective-permute-start(f32[4,64,1024]{2,1,0:T(8,128)S(1)} %get-tuple-element.18), channel_id=1, source_target_pairs={{0,1},{1,0},{2,3},{3,2},{4,5},{5,4},{6,7},{7,6},{8,9},{9,8},{10,11... | collective-permute-start | bytes 3145736 | tf_op jit(solution)/shard_map/ppermute | solution.py:38
  116.1 17.1 %collective-permute-start.24 = (f32[64,1024]{1,0:T(8,128)S(1)}, f32[64,1024]{1,0:T(8,128)S(1)}, u32[]{:S(2)}, u32[]{:S(2)}) collective-permute-start(f32[64,1024]{1,0:T(8,128)S(1)} %get-tuple-element.41), channel_id=1, source_target_pairs={{0,32},{1,56},{2,64},{3,88},{4,96},{5,120},{6,0},{7,24},{8,40},{9,... | collective-permute-start | bytes 786440 | tf_op jit(solution)/shard_map/ppermute | solution.py:56
  118.0 15.2 %collective-permute-start.26 = (f32[64,1024]{1,0:T(8,128)S(1)}, f32[64,1024]{1,0:T(8,128)S(1)}, u32[]{:S(2)}, u32[]{:S(2)}) collective-permute-start(f32[64,1024]{1,0:T(8,128)S(1)} %get-tuple-element.42), channel_id=1, source_target_pairs={{0,96},{1,120},{2,0},{3,24},{4,32},{5,56},{6,64},{7,88},{8,104},{9... | collective-permute-start | bytes 786440 | tf_op jit(solution)/shard_map/ppermute | solution.py:56
  122.2 13.1 %collective-permute-start.25 = (f32[64,1024]{1,0:T(8,128)S(1)}, f32[64,1024]{1,0:T(8,128)S(1)}, u32[]{:S(2)}, u32[]{:S(2)}) collective-permute-start(f32[64,1024]{1,0:T(8,128)S(1)} %get-tuple-element.43), channel_id=1, source_target_pairs={{0,64},{1,88},{2,96},{3,120},{4,0},{5,24},{6,32},{7,56},{8,72},{9,... | collective-permute-start | bytes 786440 | tf_op jit(solution)/shard_map/ppermute | solution.py:56
  131.3 8.3 %collective-permute-start.23 = (f32[64,1024]{1,0:T(8,128)S(1)}, f32[64,1024]{1,0:T(8,128)S(1)}, u32[]{:S(2)}, u32[]{:S(2)}) collective-permute-start(f32[64,1024]{1,0:T(8,128)S(1)} %get-tuple-element.44), channel_id=1, source_target_pairs={{0,0},{1,24},{2,32},{3,56},{4,64},{5,88},{6,96},{7,120},{8,8},{9,1... | collective-permute-start | bytes 786440 | tf_op jit(solution)/shard_map/ppermute | solution.py:56
  139.7 5.0 %collective-permute-start.36 = (f32[32,1024]{1,0:T(8,128)S(1)}, f32[32,1024]{1,0:T(8,128)S(1)}, u32[]{:S(2)}, u32[]{:S(2)}) collective-permute-start(f32[32,1024]{1,0:T(8,128)S(1)} %get-tuple-element.45), channel_id=1, source_target_pairs={{0,96},{8,104},{16,112},{24,120},{32,0},{40,8},{48,16},{56,24},{64... | collective-permute-start | bytes 393224 | tf_op jit(solution)/shard_map/ppermute | solution.py:34
  141.8 6.8 %collective-permute-start.35 = (f32[32,1024]{1,0:T(8,128)S(1)}, f32[32,1024]{1,0:T(8,128)S(1)}, u32[]{:S(2)}, u32[]{:S(2)}) collective-permute-start(f32[32,1024]{1,0:T(8,128)S(1)} %get-tuple-element.45), channel_id=1, source_target_pairs={{0,32},{8,40},{16,48},{24,56},{32,64},{40,72},{48,80},{56,88},{64,... | collective-permute-start | bytes 393224 | tf_op jit(solution)/shard_map/ppermute | solution.py:34
  141.8 6.8 %collective-permute-start.28 = (f32[32,1024]{1,0:T(8,128)S(1)}, f32[32,1024]{1,0:T(8,128)S(1)}, u32[]{:S(2)}, u32[]{:S(2)}) collective-permute-start(f32[32,1024]{1,0:T(8,128)S(1)} %get-tuple-element.48), channel_id=1, source_target_pairs={{0,24},{8,0},{16,8},{24,16},{32,56},{40,32},{48,40},{56,48},{64,88... | collective-permute-start | bytes 393224 | tf_op jit(solution)/shard_map/ppermute | solution.py:34
  143.5 6.5 %collective-permute-start.27 = (f32[32,1024]{1,0:T(8,128)S(1)}, f32[32,1024]{1,0:T(8,128)S(1)}, u32[]{:S(2)}, u32[]{:S(2)}) collective-permute-start(f32[32,1024]{1,0:T(8,128)S(1)} %get-tuple-element.48), channel_id=1, source_target_pairs={{0,8},{8,16},{16,24},{24,0},{32,40},{40,48},{48,56},{56,32},{64,72... | collective-permute-start | bytes 393224 | tf_op jit(solution)/shard_map/ppermute | solution.py:34
  144.7 12.5 %collective-permute-start.38 = (f32[16,1024]{1,0:T(8,128)S(1)}, f32[16,1024]{1,0:T(8,128)S(1)}, u32[]{:S(2)}, u32[]{:S(2)}) collective-permute-start(f32[16,1024]{1,0:T(8,128)S(1)} %slice.175), channel_id=1, source_target_pairs={{0,96},{8,104},{16,112},{24,120},{32,0},{40,8},{48,16},{56,24},{64... | collective-permute-start | bytes 196616 | tf_op jit(solution)/shard_map/ppermute | solution.py:34
  148.6 8.6 %collective-permute-start.37 = (f32[16,1024]{1,0:T(8,128)S(1)}, f32[16,1024]{1,0:T(8,128)S(1)}, u32[]{:S(2)}, u32[]{:S(2)}) collective-permute-start(f32[16,1024]{1,0:T(8,128)S(1)} %slice.174), channel_id=1, source_target_pairs={{0,32},{8,40},{16,48},{24,56},{32,64},{40,72},{48,80},{56,88},{64,... | collective-permute-start | bytes 196616 | tf_op jit(solution)/shard_map/ppermute | solution.py:34
  148.6 6.1 %collective-permute-start.30 = (f32[16,1024]{1,0:T(8,128)S(1)}, f32[16,1024]{1,0:T(8,128)S(1)}, u32[]{:S(2)}, u32[]{:S(2)}) collective-permute-start(f32[16,1024]{1,0:T(8,128)S(1)} %slice.170), channel_id=1, source_target_pairs={{0,24},{8,0},{16,8},{24,16},{32,56},{40,32},{48,40},{56,48},{64,88... | collective-permute-start | bytes 196616 | tf_op jit(solution)/shard_map/ppermute | solution.py:34
  150.1 4.7 %collective-permute-start.29 = (f32[16,1024]{1,0:T(8,128)S(1)}, f32[16,1024]{1,0:T(8,128)S(1)}, u32[]{:S(2)}, u32[]{:S(2)}) collective-permute-start(f32[16,1024]{1,0:T(8,128)S(1)} %slice.169), channel_id=1, source_target_pairs={{0,8},{8,16},{16,24},{24,0},{32,40},{40,48},{48,56},{56,32},{64,72... | collective-permute-start | bytes 196616 | tf_op jit(solution)/shard_map/ppermute | solution.py:34
  154.8 16.7 %copy-start.13 = (f32[128,1024]{1,0:T(8,128)}, f32[128,1024]{1,0:T(8,128)S(1)}, u32[]{:S(2)}) copy-start(f32[128,1024]{1,0:T(8,128)S(1)} %constant_dynamic-update-slice_fusion.10) | copy-start | bytes 1572868
  154.8 10.8 %collective-permute-start.32 = (f32[4,32,1024]{2,1,0:T(8,128)S(1)}, f32[4,32,1024]{2,1,0:T(8,128)S(1)}, u32[]{:S(2)}, u32[]{:S(2)}) collective-permute-start(f32[4,32,1024]{2,1,0:T(8,128)S(1)} %bitcast.39), channel_id=1, source_target_pairs={{0,96},{8,104},{16,112},{24,120},{32,0},{40,8},{48,16},{56,24},{64... | collective-permute-start | bytes 1572872 | tf_op jit(solution)/shard_map/ppermute | solution.py:34
  157.2 12.5 %collective-permute-start.31 = (f32[4,32,1024]{2,1,0:T(8,128)S(1)}, f32[4,32,1024]{2,1,0:T(8,128)S(1)}, u32[]{:S(2)}, u32[]{:S(2)}) collective-permute-start(f32[4,32,1024]{2,1,0:T(8,128)S(1)} %bitcast.40), channel_id=1, source_target_pairs={{0,32},{8,40},{16,48},{24,56},{32,64},{40,72},{48,80},{56,88},{64,... | collective-permute-start | bytes 1572872 | tf_op jit(solution)/shard_map/ppermute | solution.py:34
  157.3 15.0 %copy-start.14 = (f32[128,1024]{1,0:T(8,128)}, f32[128,1024]{1,0:T(8,128)S(1)}, u32[]{:S(2)}) copy-start(f32[128,1024]{1,0:T(8,128)S(1)} %constant_dynamic-update-slice_fusion.15) | copy-start | bytes 1572868
  157.3 13.2 %collective-permute-start.40 = (f32[4,32,1024]{2,1,0:T(8,128)S(1)}, f32[4,32,1024]{2,1,0:T(8,128)S(1)}, u32[]{:S(2)}, u32[]{:S(2)}) collective-permute-start(f32[4,32,1024]{2,1,0:T(8,128)S(1)} %bitcast.42), channel_id=1, source_target_pairs={{0,24},{8,0},{16,8},{24,16},{32,56},{40,32},{48,40},{56,48},{64,88... | collective-permute-start | bytes 1572872 | tf_op jit(solution)/shard_map/ppermute | solution.py:34
  157.4 14.1 %collective-permute-start.39 = (f32[4,32,1024]{2,1,0:T(8,128)S(1)}, f32[4,32,1024]{2,1,0:T(8,128)S(1)}, u32[]{:S(2)}, u32[]{:S(2)}) collective-permute-start(f32[4,32,1024]{2,1,0:T(8,128)S(1)} %bitcast.43), channel_id=1, source_target_pairs={{0,8},{8,16},{16,24},{24,0},{32,40},{40,48},{48,56},{56,32},{64,72... | collective-permute-start | bytes 1572872 | tf_op jit(solution)/shard_map/ppermute | solution.py:34
  165.6 13.4 %copy-start.6 = (f32[4,32,1024]{2,1,0:T(8,128)}, f32[4,32,1024]{2,1,0:T(8,128)S(1)}, u32[]{:S(2)}) copy-start(f32[4,32,1024]{2,1,0:T(8,128)S(1)} %collective-permute-done.32.refs_3_) | copy-start | bytes 1572868
  166.4 7.8 %collective-permute-start.34 = (f32[2,32,1024]{2,1,0:T(8,128)}, f32[2,32,1024]{2,1,0:T(8,128)S(1)}, u32[]{:S(2)}, u32[]{:S(2)}) collective-permute-start(f32[2,32,1024]{2,1,0:T(8,128)} %slice.172), channel_id=1, source_target_pairs={{0,96},{8,104},{16,112},{24,120},{32,0},{40,8},{48,16},{56,24},{64... | collective-permute-start | bytes 786440 | tf_op jit(solution)/shard_map/ppermute | solution.py:34
  169.7 9.3 %copy-start.7 = (f32[4,32,1024]{2,1,0:T(8,128)}, f32[4,32,1024]{2,1,0:T(8,128)S(1)}, u32[]{:S(2)}) copy-start(f32[4,32,1024]{2,1,0:T(8,128)S(1)} %collective-permute-done.31.refs_2_) | copy-start | bytes 1572868
  170.5 6.7 %collective-permute-start.33 = (f32[2,32,1024]{2,1,0:T(8,128)}, f32[2,32,1024]{2,1,0:T(8,128)}, u32[]{:S(2)}, u32[]{:S(2)}) collective-permute-start(f32[2,32,1024]{2,1,0:T(8,128)} %slice.171), channel_id=1, source_target_pairs={{0,32},{8,40},{16,48},{24,56},{32,64},{40,72},{48,80},{56,88},{64,... | collective-permute-start | bytes 786440 | tf_op jit(solution)/shard_map/ppermute | solution.py:34
  170.5 8.5 %copy-start.8 = (f32[4,32,1024]{2,1,0:T(8,128)}, f32[4,32,1024]{2,1,0:T(8,128)S(1)}, u32[]{:S(2)}) copy-start(f32[4,32,1024]{2,1,0:T(8,128)S(1)} %collective-permute-done.40.refs_8_) | copy-start | bytes 1572868
  171.3 6.0 %collective-permute-start.42 = (f32[2,32,1024]{2,1,0:T(8,128)}, f32[2,32,1024]{2,1,0:T(8,128)}, u32[]{:S(2)}, u32[]{:S(2)}) collective-permute-start(f32[2,32,1024]{2,1,0:T(8,128)} %slice.177), channel_id=1, source_target_pairs={{0,24},{8,0},{16,8},{24,16},{32,56},{40,32},{48,40},{56,48},{64,88... | collective-permute-start | bytes 786440 | tf_op jit(solution)/shard_map/ppermute | solution.py:34
  172.2 6.7 %collective-permute-start.41 = (f32[2,32,1024]{2,1,0:T(8,128)}, f32[2,32,1024]{2,1,0:T(8,128)}, u32[]{:S(2)}, u32[]{:S(2)}) collective-permute-start(f32[2,32,1024]{2,1,0:T(8,128)} %slice.176), channel_id=1, source_target_pairs={{0,8},{8,16},{16,24},{24,0},{32,40},{40,48},{48,56},{56,32},{64,72... | collective-permute-start | bytes 786440 | tf_op jit(solution)/shard_map/ppermute | solution.py:34
  190.8 7.9 %collective-permute-start.43 = (f32[2048,128]{1,0:T(8,128)}, f32[2048,128]{1,0:T(8,128)S(1)}, u32[]{:S(2)}, u32[]{:S(2)}) collective-permute-start(f32[2048,128]{1,0:T(8,128)} %get-tuple-element.22), channel_id=1, source_target_pairs={{0,1},{1,0},{2,3},{3,2},{4,5},{5,4},{6,7},{7,6},{8,9},{9,8},{10,11... | collective-permute-start | bytes 3145736 | tf_op jit(solution)/shard_map/ppermute | solution.py:38
  211.9 4.9 %collective-permute-start.44 = (f32[2048,128]{1,0:T(8,128)}, f32[2048,128]{1,0:T(8,128)S(1)}, u32[]{:S(2)}, u32[]{:S(2)}) collective-permute-start(f32[2048,128]{1,0:T(8,128)} %get-tuple-element.24), channel_id=1, source_target_pairs={{0,1},{1,0},{2,3},{3,2},{4,5},{5,4},{6,7},{7,6},{8,9},{9,8},{10,11... | collective-permute-start | bytes 3145736 | tf_op jit(solution)/shard_map/ppermute | solution.py:38
  212.3 4.6 %collective-permute-start.45 = (f32[2048,128]{1,0:T(8,128)}, f32[2048,128]{1,0:T(8,128)}, u32[]{:S(2)}, u32[]{:S(2)}) collective-permute-start(f32[2048,128]{1,0:T(8,128)} %get-tuple-element.26), channel_id=1, source_target_pairs={{0,1},{1,0},{2,3},{3,2},{4,5},{5,4},{6,7},{7,6},{8,9},{9,8},{10,11... | collective-permute-start | bytes 3145736 | tf_op jit(solution)/shard_map/ppermute | solution.py:38
  214.1 14.6 %collective-permute-start.47 = (f32[1024,128]{1,0:T(8,128)}, f32[1024,128]{1,0:T(8,128)}, u32[]{:S(2)}, u32[]{:S(2)}) collective-permute-start(f32[1024,128]{1,0:T(8,128)} %get-tuple-element.39), channel_id=1, source_target_pairs={{0,2},{1,3},{2,4},{3,5},{4,6},{5,7},{6,0},{7,1},{8,10},{9,11},{10,... | collective-permute-start | bytes 1572872 | tf_op jit(solution)/shard_map/ppermute | solution.py:34
  216.4 14.9 %collective-permute-start.51 = (f32[1024,128]{1,0:T(8,128)}, f32[1024,128]{1,0:T(8,128)}, u32[]{:S(2)}, u32[]{:S(2)}) collective-permute-start(f32[1024,128]{1,0:T(8,128)} %get-tuple-element.40), channel_id=1, source_target_pairs={{0,6},{1,7},{2,0},{3,1},{4,2},{5,3},{6,4},{7,5},{8,14},{9,15},{10,... | collective-permute-start | bytes 1572872 | tf_op jit(solution)/shard_map/ppermute | solution.py:34
  227.1 8.2 %copy-start.12 = (f32[2048,128]{1,0:T(8,128)S(1)}, f32[2048,128]{1,0:T(8,128)}, u32[]{:S(2)}) copy-start(f32[2048,128]{1,0:T(8,128)} %get-tuple-element.27) | copy-start | bytes 3145732
  227.1 8.2 %collective-permute-start.46 = (f32[2048,128]{1,0:T(8,128)}, f32[2048,128]{1,0:T(8,128)S(1)}, u32[]{:S(2)}, u32[]{:S(2)}) collective-permute-start(f32[2048,128]{1,0:T(8,128)} %get-tuple-element.28), channel_id=1, source_target_pairs={{0,1},{1,0},{2,3},{3,2},{4,5},{5,4},{6,7},{7,6},{8,9},{9,8},{10,11... | collective-permute-start | bytes 3145736 | tf_op jit(solution)/shard_map/ppermute | solution.py:38
  229.9 13.5 %collective-permute-start.48 = (f32[1024,128]{1,0:T(8,128)S(1)}, f32[1024,128]{1,0:T(8,128)S(1)}, u32[]{:S(2)}, u32[]{:S(2)}) collective-permute-start(f32[1024,128]{1,0:T(8,128)S(1)} %get-tuple-element.37), channel_id=1, source_target_pairs={{0,2},{1,3},{2,4},{3,5},{4,6},{5,7},{6,0},{7,1},{8,10},{9,11},{10,... | collective-permute-start | bytes 1572872 | tf_op jit(solution)/shard_map/ppermute | solution.py:34
  231.0 23.6 %collective-permute-start.50 = (f32[1024,128]{1,0:T(8,128)S(1)}, f32[1024,128]{1,0:T(8,128)S(1)}, u32[]{:S(2)}, u32[]{:S(2)}) collective-permute-start(f32[1024,128]{1,0:T(8,128)S(1)} %get-tuple-element.38), channel_id=1, source_target_pairs={{0,2},{1,3},{2,4},{3,5},{4,6},{5,7},{6,0},{7,1},{8,10},{9,11},{10,... | collective-permute-start | bytes 1572872 | tf_op jit(solution)/shard_map/ppermute | solution.py:34
  232.4 22.2 %collective-permute-start.49 = (f32[1024,128]{1,0:T(8,128)S(1)}, f32[1024,128]{1,0:T(8,128)S(1)}, u32[]{:S(2)}, u32[]{:S(2)}) collective-permute-start(f32[1024,128]{1,0:T(8,128)S(1)} %get-tuple-element.35), channel_id=1, source_target_pairs={{0,6},{1,7},{2,0},{3,1},{4,2},{5,3},{6,4},{7,5},{8,14},{9,15},{10,... | collective-permute-start | bytes 1572872 | tf_op jit(solution)/shard_map/ppermute | solution.py:34
  234.9 20.8 %collective-permute-start.52 = (f32[1024,128]{1,0:T(8,128)S(1)}, f32[1024,128]{1,0:T(8,128)S(1)}, u32[]{:S(2)}, u32[]{:S(2)}) collective-permute-start(f32[1024,128]{1,0:T(8,128)S(1)} %get-tuple-element.36), channel_id=1, source_target_pairs={{0,6},{1,7},{2,0},{3,1},{4,2},{5,3},{6,4},{7,5},{8,14},{9,15},{10,... | collective-permute-start | bytes 1572872 | tf_op jit(solution)/shard_map/ppermute | solution.py:34
  (7 other events, 23.1 us)

commit v2 on v1

--- a/solution.py
+++ b/solution.py
@@ -56,23 +56,23 @@
     return lax.ppermute(value, ("row", "col"), scatter_pairs(turn))
 
 
-def gather_line(block, axis):
-    half = block.shape[0] // 2
-    before = move(block, axis, 1)
-    after = move(block, axis, -1)
-    far_low = move(before[:half], axis, 1)
-    far_high = move(after[half:], axis, -1)
-    return block, before, after, far_low, far_high
+def gather_line(low, high, axis):
+    before_low, after_high = move(low, axis, 1), move(high, axis, -1)
+    before_high, after_low = move(high, axis, 1), move(low, axis, -1)
+    far_low, far_high = move(before_low, axis, 1), move(after_high, axis, -1)
+    return low, high, before_low, before_high, after_low, after_high, far_low, far_high
+
+
+def line_halves(block, axis):
+    before, after, far = move(block, axis, 1), move(block, axis, -1), move(block, axis, 2)
+    return jnp.stack([block, before]), jnp.stack([after, far])
 
 
 def gather_plane(block):
     half = block.shape[0] // 2
-    first = gather_line(block[:half], "x")
-    second = gather_line(block[half:], "y")
-    shape = (SIDE, half) + block.shape[1:]
-    first = jnp.concatenate(first, axis=0).reshape(shape)
-    second = jnp.concatenate(second, axis=0).reshape(shape)
-    return gather_line(first, "y") + gather_line(second, "x")
+    first = line_halves(block[:half], "x")
+    second = line_halves(block[half:], "y")
+    return gather_line(*first, "y") + gather_line(*second, "x")
 
 
 def plane_order(my_row, my_col):
@@ -113,9 +113,9 @@
 
 
 def pair_kernel(order, panel_order, *refs):
-    first, second, panels = refs[:5], refs[5:10], refs[10:15]
-    coulomb, keep, send = refs[15:18]
-    column, panel, p_high, p_low, total, column_sem, panel_sem = refs[18:]
+    first, second, panels = refs[:8], refs[8:16], refs[16:24]
+    coulomb, keep, send = refs[24:27]
+    column, panel, p_high, p_low, total, column_sem, panel_sem = refs[27:]
     rows = first[0].shape[1]
     lanes = first[0].shape[2]
     panel_copies = []
@@ -172,7 +172,7 @@
     return pl.pallas_call(
         pair_kernel,
         out_shape=(out, out),
-        in_specs=[scalars, scalars] + [anywhere] * 15 + [vmem],
+        in_specs=[scalars, scalars] + [anywhere] * 24 + [vmem],
         out_specs=(vmem, vmem),
         scratch_shapes=[
             pltpu.VMEM((width, bands), F32),
@@ -189,14 +189,13 @@
     )(order, panel_order, *column_pieces, *panel_pieces, coulomb)
 
 
-def term_kernel(groups, gathered, where, *refs):
-    refs = list(refs)
+def term_kernel(gathered, where, *refs):
+    tile = pl.program_id(0)
     if gathered:
-        order, first, second = refs[0], refs[1:6], refs[6:11]
-        refs = refs[11:]
-        outs, (high, low, whole, sem) = refs[1:-4], refs[-4:]
-
-        @pl.when(pl.program_id(0) == 0)
+        order, first, second = refs[0], refs[1:9], refs[9:17]
+        fitting, outs, (high, low, whole, sem) = refs[17], refs[18:22], refs[22:]
+
+        @pl.when(tile == 0)
         def _():
             rows = first[0].shape[1]
             copies = []
@@ -215,52 +214,55 @@
                 copy.wait()
             high[...], low[...] = split(whole[...])
     else:
-        weights, outs = refs[1 : 1 + 2 * groups], refs[2 + 2 * groups :]
-    f_high, f_low = split(refs[0][...])
-    even = where[SIDE] == 0
-    half = outs[0].shape[1]
-    bands = 2 * half
-    for group in range(groups):
+        fitting, weights, outs = refs[0], refs[1:5], refs[7:11]
+    f_high, f_low = split(fitting[...])
+    even = where[3] == 0
+    half = outs[0].shape[2]
+    for group in range(2):
         if gathered:
-            here = pl.ds(pl.multiple_of(where[group] * bands, bands), bands)
+            start = chip_of(group, tile, where) * 2 * half
+            here = pl.ds(pl.multiple_of(start, 2 * half), 2 * half)
             w_high, w_low = high[:, here], low[:, here]
         else:
             w_high, w_low = weights[2 * group][...], weights[2 * group + 1][...]
         product = dot3(f_high, f_low, w_high, w_low, ((1,), (0,)))
         lower, upper = product[:, :half], product[:, half:]
-        outs[2 * group][...] = jnp.where(even, lower, upper)
-        outs[2 * group + 1][...] = jnp.where(even, upper, lower)
-
-
-def term(groups, where, fitting, weights=None, after=None, order=None, pieces=None):
+        outs[2 * group][0] = jnp.where(even, lower, upper)
+        outs[2 * group + 1][0] = jnp.where(even, upper, lower)
+
+
+def chip_of(group, tile, where):
+    return where[0] if group == 0 else jnp.where(tile < 2, where[1], where[2])
+
+
+def term(where, fitting, gathered=None, weights=None, after=None):
     rows, points = fitting.shape
     bands = 8 * 128
-    tile = 512
-    gathered = pieces is not None
-    halves = 2 * groups
+    tile = rows // 4
     anywhere = pl.BlockSpec(memory_space=pltpu.HBM)
     streamed = pl.BlockSpec((tile, points), lambda i, where: (i, 0))
     resident = pl.BlockSpec((points, bands), lambda i, where: (0, 0), pipeline_mode=pl.Buffered(1))
-    half = pl.BlockSpec((tile, bands // 8), lambda i, where: (i, 0))
-    out = [jax.ShapeDtypeStruct((rows, bands // 8), F32)] * halves
-    out_specs = [half] * halves
+    half = pl.BlockSpec((1, tile, bands // 8), lambda i, where: (i // 2, lax.rem(i, 2), 0))
+    out = [jax.ShapeDtypeStruct((2, rows // 2, bands // 8), F32)] * 4
+    out_specs = [half] * 4
     scratch = []
-    if gathered:
-        in_specs = [pl.BlockSpec(memory_space=pltpu.SMEM)] + [anywhere] * 10 + [streamed]
-        operands = (order, *pieces, fitting)
+    if gathered is not None:
+        in_specs = [pl.BlockSpec(memory_space=pltpu.SMEM)] + [anywhere] * 16 + [streamed]
+        operands = (*gathered, fitting)
         out += [jax.ShapeDtypeStruct((points, bands), BF16)] * 2
         out_specs += [resident] * 2
         scratch = [pltpu.VMEM((points, bands), F32), pltpu.SemaphoreType.DMA((32,))]
     else:
-        in_specs, operands = [streamed], [fitting]
-        for group in range(groups):
-            chosen = pl.BlockSpec((points, bands // SIDE), lambda i, where, group=group: (0, where[group]))
+        in_specs = [streamed]
+        for group in range(2):
+            chosen = pl.BlockSpec(
+                (points, bands // SIDE), lambda i, where, group=group: (0, chip_of(group, i, where))
+            )
             in_specs += [chosen, chosen]
-            operands += weights
-        in_specs.append(anywhere)
-        operands.append(after)
+        in_specs += [anywhere] * 2
+        operands = (fitting, *weights, *weights, *after)
     return pl.pallas_call(
-        functools.partial(term_kernel, groups, gathered),
+        functools.partial(term_kernel, gathered is not None),
         out_shape=out,
         grid_spec=pltpu.PrefetchScalarGridSpec(
             num_scalar_prefetch=1,
@@ -270,7 +272,7 @@
             scratch_shapes=scratch,
         ),
         cost_estimate=pl.CostEstimate(
-            flops=6 * groups * rows * points * bands // SIDE, bytes_accessed=11 << 20, transcendentals=0
+            flops=12 * rows * points * bands // SIDE, bytes_accessed=16 << 20, transcendentals=0
         ),
         name="term",
     )(where, *operands)
@@ -307,9 +309,8 @@
     strip = picked_strip(orbitals, point_index, my_row)
 
     column_pieces = gather_plane(to_plane(strip, 0))
-    both = jnp.stack([strip, swap_cores(strip)])
-    before, after = move(both, "z", 1), move(both, "z", -1)
-    panel_pieces = (both, before, after, move(before[:1], "z", 1), move(after[1:], "z", -1))
+    panel = strip.reshape((1,) + strip.shape)
+    panel_pieces = gather_line(panel, swap_cores(panel), "z")
     place = jnp.array(REL, jnp.int32).repeat(2)
     cores = jnp.tile(jnp.array([0, 1], jnp.int32), SIDE)
     panel_order = jnp.concatenate(
@@ -323,27 +324,30 @@
     pieces = gather_plane(w_strip)
 
     def targets(*steps):
-        chips = [(height + step) % SIDE for step in steps] + [height] * (SIDE - len(steps))
-        return jnp.stack(chips + [core]).astype(jnp.int32)
-
-    half = fitting.shape[0] // 2
-    mine, other, *weights = term(1, targets(2), fitting, order=order, pieces=pieces)
-    far = mine + swap_cores(other)
-    far_up = move(far[:half], "z", 1)
-    far_down = move(far[half:], "z", -1)
-    chips, tag = targets(1, -1), far[:8]
-    mine, other, mine_down, other_down = term(2, chips, fitting, weights, tag)
-    up = mine + swap_cores(other)
-    down = mine_down + swap_cores(other_down)
-    up_high = move(up[half:], "z", 1)
-    down_low = move(down[:half], "z", -1)
-    up_low = move(up[:half] + far_up, "z", 1)
-    down_high = move(down[half:] + far_down, "z", -1)
-    chips, tag = targets(0), up[:8] + down[:8]
-    mine, other = term(1, chips, fitting, weights, tag)
-    own = mine + swap_cores(other)
-    low = own[:half] + (up_low + down_low)
-    high = own[half:] + (up_high + down_high)
+        chips = [(height + step) % SIDE for step in steps]
+        return jnp.stack(chips + [core, core, core]).astype(jnp.int32)
+
+    far_chips, own_chips = targets(2, -1, 1), targets(0, 1, -1)
+
+    def both_cores(mine, other):
+        other = swap_cores(other)
+        return mine[0] + other[0], mine[1] + other[1]
+
+    mine_far, other_far, mine, other, *weights = term(far_chips, fitting, gathered=(order, *pieces))
+    far_low, far_high = both_cores(mine_far, other_far)
+    far_up = move(far_low, "z", 1)
+    far_down = move(far_high, "z", -1)
+    down_low, up_high = both_cores(mine, other)
+    after = (down_low, up_high)
+    up_high = move(up_high, "z", 1)
+    down_low = move(down_low, "z", -1)
+    mine_own, other_own, mine, other = term(own_chips, fitting, weights=weights, after=after)
+    up_low, down_high = both_cores(mine, other)
+    up_low = move(up_low + far_up, "z", 1)
+    down_high = move(down_high + far_down, "z", -1)
+    own_low, own_high = both_cores(mine_own, other_own)
+    low = own_low + (up_low + down_low)
+    high = own_high + (up_high + down_high)
     return -jnp.concatenate([low, high], axis=0)
 
 

time: 259 us -> 254 us (0.981)
  starting transfers between devices: 94.4 us -> 106 us
  local copies, waits for them, and re-layouts: 22.3 us -> 15.9 us
  Pallas kernels: 47.6 us -> 41.8 us
  other arithmetic: 9.97 us -> 5.8 us
    ppermute x42 -> x48, starting transfers between devices: 47.1 us -> 69 us  [move(): return lax.ppermute(value, name, pairs)]
    slice x22 -> x0, local copies, waits for them, and re-layouts: 9.29 us -> none  [the longest x8 3.52 us: gather_line(): far_low = move(before[:half], axis, 1)]
    ppermute x6, starting transfers between devices: 18.4 us -> 11.8 us  [swap_cores(): return lax.ppermute(value, 'col', [(c, c ^ 1) for c in range(2 * SIDE)])]
    pallas_call x3 -> x2, Pallas kernels: 31.3 us -> 25.9 us  [term(): pl.pallas_call(functools.partial(term_kernel, gathered is not None), out_...]
    ppermute x5, waiting for transfers between devices: 10.4 us -> 5.4 us  [to_plane(): return lax.ppermute(value, ('row', 'col'), scatter_pairs(turn))]
    ppermute x42 -> x48, waiting for transfers between devices: 56.9 us -> 61.6 us  [move(): return lax.ppermute(value, name, pairs)]
    unnamed x46 -> x60, local copies, waits for them, and re-layouts: 4.52 us -> 8.52 us
    ppermute x5, starting transfers between devices: 21.2 us -> 17.8 us  [to_plane(): return lax.ppermute(value, ('row', 'col'), scatter_pairs(turn))]
  transfers between devices with their start and end apart: 54 -> 60, of which waited for: 22 -> 28; matrix products, arithmetic and copies ran while one was open for 8% -> 2% of each run, Pallas kernels for 3% -> 5%
where the time goes in v2:
time: 254 us; the launch traced here: 252 us
  starting transfers between devices  106 us (42%)
  waiting for transfers between devices  81.2 us (32%)
  Pallas kernels  41.8 us (16%)
  local copies, waits for them, and re-layouts  15.9 us (6%)
  other arithmetic  5.8 us (2%)
    ppermute x48, starting transfers between devices, move(): return lax.ppermute(value, name, pairs)  69 us
    ppermute x48, waiting for transfers between devices, move(): return lax.ppermute(value, name, pairs)  61.6 us
    pallas_call x2, Pallas kernels, term(): pl.pallas_call(functools.partial(term_kernel, gathered is not None), out_...  25.9 us
    ppermute x5, starting transfers between devices, to_plane(): return lax.ppermute(value, ('row', 'col'), scatter_pairs(turn))  17.8 us
    pallas_call x1, Pallas kernels, pair_weights(): pl.pallas_call(pair_kernel, out_shape=(out, out), in_specs=[scalars, scal...  16 us
    ppermute x6, starting transfers between devices, swap_cores(): return lax.ppermute(value, 'col', [(c, c ^ 1) for c in range(2 * SIDE)])  11.8 us
    all_to_all x1, waiting for transfers between devices, picked_strip(): lax.all_to_all(outgoing, 'row', split_axis=0, concat_axis=0, tiled=True)  10.2 us
    unnamed x60, local copies, waits for them, and re-layouts  8.52 us
  transfers between devices with their start and end apart: 60, of which 28 were waited for; matrix products, arithmetic and copies ran while one was open for 2% of the time, Pallas kernels for 5%

profile of v2, /device:TPU:1, one launch (start us, length us, event | category | flops | bytes accessed | tf_op | source)
XLA Modules:
  0.0 252.2 jit_solution(12259894513302917653)
XLA Ops:
  1.8 4.0 %gather_fusion = f32[1024,128]{1,0:T(8,128)} fusion(f32[2048,128]{1,0:T(8,128)S(1)} %copy-done, s32[1024]{0:T(1024)S(1)} %broadcast_clamp_fusion), kind=kCustom, calls=%fused_computation | custom fusion | bytes 1052672 | tf_op jit(solution)/shard_map/gather | solution.py:295
  5.8 7.7 %all-to-all-start = ((f32[16,64,128]{2,1,0:T(8,128)}), f32[16,64,128]{2,1,0:T(8,128)S(1)}, u32[]{:S(2)}, u32[]{:S(2)}) async-start(f32[16,64,128]{2,1,0:T(8,128)} %bitcast.7), calls=%async_computation | async-start | bytes 1048576 | tf_op jit(solution)/shard_map/all_to_all | solution.py:296
  13.8 10.2 %all-to-all-done = f32[16,64,128]{2,1,0:T(8,128)S(1)} async-done(((f32[16,64,128]{2,1,0:T(8,128)}), f32[16,64,128]{2,1,0:T(8,128)S(1)}, u32[]{:S(2)}, u32[]{:S(2)}) %all-to-all-start) | async-done | bytes 524320 | tf_op jit(solution)/shard_map/all_to_all | solution.py:296
  23.9 1.0 gather_fusion.1
  25.0 4.1 %collective-permute-start = (f32[512,128]{1,0:T(8,128)S(1)}, f32[512,128]{1,0:T(8,128)S(1)}, u32[]{:S(2)}, u32[]{:S(2)}) collective-permute-start(f32[512,128]{1,0:T(8,128)S(1)} %gather_fusion.1), channel_id=1, source_target_pairs={{0,0},{1,24},{2,32},{3,56},{4,64},{5,88},{6,96},{7,120},{8,8},{9,1... | collective-permute-start | bytes 786440 | tf_op jit(solution)/shard_map/ppermute | solution.py:56
  29.1 3.1 %collective-permute-start.22 = (f32[1,512,128]{2,1,0:T(8,128)S(1)}, f32[1,512,128]{2,1,0:T(8,128)S(1)}, u32[]{:S(2)}, u32[]{:S(2)}) collective-permute-start(f32[1,512,128]{2,1,0:T(8,128)S(1)} %bitcast.70), channel_id=1, source_target_pairs={{0,6},{1,7},{2,0},{3,1},{4,2},{5,3},{6,4},{7,5},{8,14},{9,15},{10,... | collective-permute-start | bytes 786440 | tf_op jit(solution)/shard_map/ppermute | solution.py:34
  33.6 1.2 collective-permute-start.1
  34.9 2.4 collective-permute-done.22.refs_20_
  37.3 3.1 %collective-permute-done.20.refs_18_ = f32[1,512,128]{2,1,0:T(8,128)S(1)} collective-permute-done((f32[1,512,128]{2,1,0:T(8,128)S(1)}, f32[1,512,128]{2,1,0:T(8,128)S(1)}, u32[]{:S(2)}, u32[]{:S(2)}) %collective-permute-start.20) | collective-permute-done | bytes 262176 | tf_op jit(solution)/shard_map/ppermute | solution.py:34
  40.5 7.4 %collective-permute-start.11 = (f32[256,128]{1,0:T(8,128)S(1)}, f32[256,128]{1,0:T(8,128)S(1)}, u32[]{:S(2)}, u32[]{:S(2)}) collective-permute-start(f32[256,128]{1,0:T(8,128)S(1)} %get-tuple-element.51), channel_id=1, source_target_pairs={{0,96},{8,104},{16,112},{24,120},{32,0},{40,8},{48,16},{56,24},{64... | collective-permute-start | bytes 393224 | tf_op jit(solution)/shard_map/ppermute | solution.py:34
  48.0 5.8 %collective-permute-start.12 = (f32[256,128]{1,0:T(8,128)S(1)}, f32[256,128]{1,0:T(8,128)S(1)}, u32[]{:S(2)}, u32[]{:S(2)}) collective-permute-start(f32[256,128]{1,0:T(8,128)S(1)} %get-tuple-element.51), channel_id=1, source_target_pairs={{0,64},{8,72},{16,80},{24,88},{32,96},{40,104},{48,112},{56,120},{... | collective-permute-start | bytes 393224 | tf_op jit(solution)/shard_map/ppermute | solution.py:34
  53.9 1.6 collective-permute-start.23
  55.5 1.5 collective-permute-start.7
  57.0 1.3 collective-permute-done.12
  58.3 2.7 %collective-permute-start.6 = (f32[2,256,128]{2,1,0:T(8,128)S(1)}, f32[2,256,128]{2,1,0:T(8,128)S(1)}, u32[]{:S(2)}, u32[]{:S(2)}) collective-permute-start(f32[2,256,128]{2,1,0:T(8,128)S(1)} %pad_maximum_fusion.refs_0_), channel_id=1, source_target_pairs={{0,96},{8,104},{16,112},{24,120},{32,0},{40,8},{48,16},{56,24},{64... | collective-permute-start | bytes 786440 | tf_op jit(solution)/shard_map/ppermute | solution.py:34
  61.1 1.6 collective-permute-done.21.refs_19_
  63.6 1.3 collective-permute-start.14
  69.2 2.3 collective-permute-done.4.refs_2_
  71.5 1.2 collective-permute-start.25
  74.8 1.9 collective-permute-start.18
  77.5 1.0 collective-permute-done.9.refs_7_
  78.5 1.7 collective-permute-done.8.refs_6_
  80.5 3.8 %collective-permute-done.17.refs_14_ = f32[2,256,128]{2,1,0:T(8,128)S(1)} collective-permute-done((f32[2,256,128]{2,1,0:T(8,128)}, f32[2,256,128]{2,1,0:T(8,128)S(1)}, u32[]{:S(2)}, u32[]{:S(2)}) %collective-permute-start.17) | collective-permute-done | bytes 262176 | tf_op jit(solution)/shard_map/ppermute | solution.py:34
  84.3 1.6 copy-done.2
  85.9 0.9 copy-done.4
  86.9 0.9 copy-done.6
  87.8 0.9 copy-done.8
  89.7 0.9 copy-done.12
  90.7 16.0 %pair_weights.1 = (f32[4,64,1024]{2,1,0:T(8,128)S(1)}, f32[4,64,1024]{2,1,0:T(8,128)S(1)}) custom-call(s32[4,16]{1,0:T(4,128)S(1)} %pad_add_fusion.order.refs_0_, s32[10]{0:T(128)S(1)} %pad_add_fusion.1.panel_order, f32[2,256,128]{2,1,0:T(8,128)S(1)} %pad_maximum_fusion.refs_0_, f32[2,256,128]{2,1,0:T(8,128)S(1)} %pad_maximum_fusion.1.refs_1_, ...), custom_call_target="tpu_custom_call" | custom-call | flops 6442450944 | bytes 12582912 | tf_op jit(solution)/shard_map/pair_weights/pallas_call | solution.py:172
  106.6 5.2 %collective-permute-start.26 = (f32[4,64,1024]{2,1,0:T(8,128)S(1)}, f32[4,64,1024]{2,1,0:T(8,128)S(1)}, u32[]{:S(2)}, u32[]{:S(2)}) collective-permute-start(f32[4,64,1024]{2,1,0:T(8,128)S(1)} %get-tuple-element.18), channel_id=1, source_target_pairs={{0,1},{1,0},{2,3},{3,2},{4,5},{5,4},{6,7},{7,6},{8,9},{9,8},{10,11... | collective-permute-start | bytes 3145736 | tf_op jit(solution)/shard_map/ppermute | solution.py:38
  111.9 2.3 collective-permute-done.26
  114.4 1.9 collective-permute-start.28
  116.3 4.4 %collective-permute-start.30 = (f32[64,1024]{1,0:T(8,128)S(1)}, f32[64,1024]{1,0:T(8,128)S(1)}, u32[]{:S(2)}, u32[]{:S(2)}) collective-permute-start(f32[64,1024]{1,0:T(8,128)S(1)} %get-tuple-element.42), channel_id=1, source_target_pairs={{0,96},{1,120},{2,0},{3,24},{4,32},{5,56},{6,64},{7,88},{8,104},{9... | collective-permute-start | bytes 786440 | tf_op jit(solution)/shard_map/ppermute | solution.py:56
  120.8 3.4 %collective-permute-start.29 = (f32[64,1024]{1,0:T(8,128)S(1)}, f32[64,1024]{1,0:T(8,128)S(1)}, u32[]{:S(2)}, u32[]{:S(2)}) collective-permute-start(f32[64,1024]{1,0:T(8,128)S(1)} %get-tuple-element.43), channel_id=1, source_target_pairs={{0,64},{1,88},{2,96},{3,120},{4,0},{5,24},{6,32},{7,56},{8,72},{9,... | collective-permute-start | bytes 786440 | tf_op jit(solution)/shard_map/ppermute | solution.py:56
  124.2 4.0 %collective-permute-start.27 = (f32[64,1024]{1,0:T(8,128)S(1)}, f32[64,1024]{1,0:T(8,128)S(1)}, u32[]{:S(2)}, u32[]{:S(2)}) collective-permute-start(f32[64,1024]{1,0:T(8,128)S(1)} %get-tuple-element.44), channel_id=1, source_target_pairs={{0,0},{1,24},{2,32},{3,56},{4,64},{5,88},{6,96},{7,120},{8,8},{9,1... | collective-permute-start | bytes 786440 | tf_op jit(solution)/shard_map/ppermute | solution.py:56
  128.2 5.4 %collective-permute-done.29 = f32[64,1024]{1,0:T(8,128)S(1)} collective-permute-done((f32[64,1024]{1,0:T(8,128)S(1)}, f32[64,1024]{1,0:T(8,128)S(1)}, u32[]{:S(2)}, u32[]{:S(2)}) %collective-permute-start.29) | collective-permute-done | bytes 262176 | tf_op jit(solution)/shard_map/ppermute | solution.py:56
  133.7 2.1 collective-permute-start.32
  136.4 5.5 %collective-permute-start.41 = (f32[32,1024]{1,0:T(8,128)S(1)}, f32[32,1024]{1,0:T(8,128)S(1)}, u32[]{:S(2)}, u32[]{:S(2)}) collective-permute-start(f32[32,1024]{1,0:T(8,128)S(1)} %get-tuple-element.47), channel_id=1, source_target_pairs={{0,96},{8,104},{16,112},{24,120},{32,0},{40,8},{48,16},{56,24},{64... | collective-permute-start | bytes 393224 | tf_op jit(solution)/shard_map/ppermute | solution.py:34
  141.9 8.6 %collective-permute-start.42 = (f32[32,1024]{1,0:T(8,128)S(1)}, f32[32,1024]{1,0:T(8,128)S(1)}, u32[]{:S(2)}, u32[]{:S(2)}) collective-permute-start(f32[32,1024]{1,0:T(8,128)S(1)} %get-tuple-element.47), channel_id=1, source_target_pairs={{0,64},{8,72},{16,80},{24,88},{32,96},{40,104},{48,112},{56,120},{... | collective-permute-start | bytes 393224 | tf_op jit(solution)/shard_map/ppermute | solution.py:34
  150.7 1.4 collective-permute-start.35
  152.2 1.4 collective-permute-start.36
  154.1 3.2 %collective-permute-start.46 = (f32[2,32,1024]{2,1,0:T(8,128)S(1)}, f32[2,32,1024]{2,1,0:T(8,128)S(1)}, u32[]{:S(2)}, u32[]{:S(2)}) collective-permute-start(f32[2,32,1024]{2,1,0:T(8,128)S(1)} %pad_maximum_fusion.7.refs_10_), channel_id=1, source_target_pairs={{0,24},{8,0},{16,8},{24,16},{32,56},{40,32},{48,40},{56,48},{64,88... | collective-permute-start | bytes 786440 | tf_op jit(solution)/shard_map/ppermute | solution.py:34
  157.5 1.0 collective-permute-done.35.refs_4_
  158.5 1.1 collective-permute-start.43
  159.6 3.2 %collective-permute-done.36.refs_5_ = f32[2,32,1024]{2,1,0:T(8,128)S(1)} collective-permute-done((f32[2,32,1024]{2,1,0:T(8,128)S(1)}, f32[2,32,1024]{2,1,0:T(8,128)S(1)}, u32[]{:S(2)}, u32[]{:S(2)}) %collective-permute-start.36) | collective-permute-done | bytes 262176 | tf_op jit(solution)/shard_map/ppermute | solution.py:34
  162.8 3.7 %collective-permute-start.45 = (f32[2,32,1024]{2,1,0:T(8,128)S(1)}, f32[2,32,1024]{2,1,0:T(8,128)}, u32[]{:S(2)}, u32[]{:S(2)}) collective-permute-start(f32[2,32,1024]{2,1,0:T(8,128)S(1)} %pad_maximum_fusion.6.refs_9_), channel_id=1, source_target_pairs={{0,24},{8,0},{16,8},{24,16},{32,56},{40,32},{48,40},{56,48},{64,88... | collective-permute-start | bytes 786440 | tf_op jit(solution)/shard_map/ppermute | solution.py:34
  166.5 1.5 collective-permute-start.39
  168.1 2.2 collective-permute-start.48
  171.0 1.2 collective-permute-done.39.refs_8_
  172.2 2.7 %collective-permute-done.38.refs_7_ = f32[2,32,1024]{2,1,0:T(8,128)} collective-permute-done((f32[2,32,1024]{2,1,0:T(8,128)S(1)}, f32[2,32,1024]{2,1,0:T(8,128)}, u32[]{:S(2)}, u32[]{:S(2)}) %collective-permute-start.38) | collective-permute-done | bytes 262176 | tf_op jit(solution)/shard_map/ppermute | solution.py:34
  174.9 1.5 collective-permute-done.48.refs_16_
  177.4 14.2 %term.2 = (f32[2,1024,128]{2,1,0:T(8,128)}, f32[2,1024,128]{2,1,0:T(8,128)}, f32[2,1024,128]{2,1,0:T(8,128)}, f32[2,1024,128]{2,1,0:T(8,128)}, bf16[1024,1024]{1,0:T(8,128)(2,1)}, /*index=5*/bf16[1024,1024]{1,0:T(8,128)(2,1)}) custom-call(s32[6]{0:T(128)} %stack.117.where, s32[4,16]{1,0:T(4,128)} %copy-done.1, f32[2,32,1024]{2,1,0:T(8,128)} %copy-done.19, ...), custom_call_target="tpu_custom_call" | custom-call | flops 6442450944 | bytes 16777216 | tf_op jit(solution)/shard_map/term/pallas_call | solution.py:264
  191.6 4.5 %collective-permute-start.49 = (f32[2,1024,128]{2,1,0:T(8,128)}, f32[2,1024,128]{2,1,0:T(8,128)S(1)}, u32[]{:S(2)}, u32[]{:S(2)}) collective-permute-start(f32[2,1024,128]{2,1,0:T(8,128)} %get-tuple-element.22), channel_id=1, source_target_pairs={{0,1},{1,0},{2,3},{3,2},{4,5},{5,4},{6,7},{7,6},{8,9},{9,8},{10,11... | collective-permute-start | bytes 3145736 | tf_op jit(solution)/shard_map/ppermute | solution.py:38
  196.8 1.8 collective-permute-done.49
  198.6 2.3 fusion.13
  200.9 11.7 %term.3 = (f32[2,1024,128]{2,1,0:T(8,128)}, f32[2,1024,128]{2,1,0:T(8,128)}, f32[2,1024,128]{2,1,0:T(8,128)}, f32[2,1024,128]{2,1,0:T(8,128)}) custom-call(s32[6]{0:T(128)} %stack.115.where, f32[2048,1024]{1,0:T(8,128)} %refs_0_.1, bf16[1024,1024]{1,0:T(8,128)(2,1)} %get-tuple-element.19.refs_1_.refs_3_, ...), custom_call_target="tpu_custom_call" | custom-call | flops 6442450944 | bytes 16777216 | tf_op jit(solution)/shard_map/term/pallas_call | solution.py:264
  213.2 1.4 collective-permute-start.53
  214.6 1.4 collective-permute-start.57
  216.8 11.1 %collective-permute-done.53 = f32[1024,128]{1,0:T(8,128)S(1)} collective-permute-done((f32[1024,128]{1,0:T(8,128)S(1)}, f32[1024,128]{1,0:T(8,128)S(1)}, u32[]{:S(2)}, u32[]{:S(2)}) %collective-permute-start.53) | collective-permute-done | bytes 524320 | tf_op jit(solution)/shard_map/ppermute | solution.py:34
  228.1 1.5 collective-permute-start.54
  229.6 1.2 collective-permute-start.58
  230.8 8.2 %collective-permute-done.56 = f32[1024,128]{1,0:T(8,128)S(1)} collective-permute-done((f32[1024,128]{1,0:T(8,128)S(1)}, f32[1024,128]{1,0:T(8,128)S(1)}, u32[]{:S(2)}, u32[]{:S(2)}) %collective-permute-start.56) | collective-permute-done | bytes 524320 | tf_op jit(solution)/shard_map/ppermute | solution.py:34
  239.7 10.6 %collective-permute-done.54 = f32[1024,128]{1,0:T(8,128)S(1)} collective-permute-done((f32[1024,128]{1,0:T(8,128)S(1)}, f32[1024,128]{1,0:T(8,128)S(1)}, u32[]{:S(2)}, u32[]{:S(2)}) %collective-permute-start.54) | collective-permute-done | bytes 524320 | tf_op jit(solution)/shard_map/ppermute | solution.py:34
  251.2 1.0 maximum_negate_fusion
  (174 shorter events, 20.2 us)
Async XLA Ops:
  5.8 26.4 %copy-start.22 = (s32[4]{0:T(128)S(1)}, s32[4]{0:T(128)}, u32[]{:S(2)}) copy-start(s32[4]{0:T(128)} %constant.150.clone) | copy-start | bytes 52
  5.8 18.1 %all-to-all-start = ((f32[16,64,128]{2,1,0:T(8,128)}), f32[16,64,128]{2,1,0:T(8,128)S(1)}, u32[]{:S(2)}, u32[]{:S(2)}) async-start(f32[16,64,128]{2,1,0:T(8,128)} %bitcast.7), calls=%async_computation | async-start | bytes 1048576 | tf_op jit(solution)/shard_map/all_to_all | solution.py:296
  25.0 8.3 %collective-permute-start = (f32[512,128]{1,0:T(8,128)S(1)}, f32[512,128]{1,0:T(8,128)S(1)}, u32[]{:S(2)}, u32[]{:S(2)}) collective-permute-start(f32[512,128]{1,0:T(8,128)S(1)} %gather_fusion.1), channel_id=1, source_target_pairs={{0,0},{1,24},{2,32},{3,56},{4,64},{5,88},{6,96},{7,120},{8,8},{9,1... | collective-permute-start | bytes 786440 | tf_op jit(solution)/shard_map/ppermute | solution.py:56
  29.1 8.2 %collective-permute-start.22 = (f32[1,512,128]{2,1,0:T(8,128)S(1)}, f32[1,512,128]{2,1,0:T(8,128)S(1)}, u32[]{:S(2)}, u32[]{:S(2)}) collective-permute-start(f32[1,512,128]{2,1,0:T(8,128)S(1)} %bitcast.70), channel_id=1, source_target_pairs={{0,6},{1,7},{2,0},{3,1},{4,2},{5,3},{6,4},{7,5},{8,14},{9,15},{10,... | collective-permute-start | bytes 786440 | tf_op jit(solution)/shard_map/ppermute | solution.py:34
  32.2 8.2 %collective-permute-start.20 = (f32[1,512,128]{2,1,0:T(8,128)S(1)}, f32[1,512,128]{2,1,0:T(8,128)S(1)}, u32[]{:S(2)}, u32[]{:S(2)}) collective-permute-start(f32[1,512,128]{2,1,0:T(8,128)S(1)} %bitcast.71), channel_id=1, source_target_pairs={{0,2},{1,3},{2,4},{3,5},{4,6},{5,7},{6,0},{7,1},{8,10},{9,11},{10,... | collective-permute-start | bytes 786440 | tf_op jit(solution)/shard_map/ppermute | solution.py:34
  32.4 21.4 %collective-permute-start.19 = (f32[1,512,128]{2,1,0:T(8,128)S(1)}, f32[1,512,128]{2,1,0:T(8,128)S(1)}, u32[]{:S(2)}, u32[]{:S(2)}) collective-permute-start(f32[1,512,128]{2,1,0:T(8,128)S(1)} %bitcast.72), channel_id=1, source_target_pairs={{0,1},{1,0},{2,3},{3,2},{4,5},{5,4},{6,7},{7,6},{8,9},{9,8},{10,11... | collective-permute-start | bytes 786440 | tf_op jit(solution)/shard_map/ppermute | solution.py:38
  33.3 7.2 %collective-permute-start.2 = (f32[256,128]{1,0:T(8,128)S(1)}, f32[256,128]{1,0:T(8,128)S(1)}, u32[]{:S(2)}, u32[]{:S(2)}) collective-permute-start(f32[256,128]{1,0:T(8,128)S(1)} %get-tuple-element.52), channel_id=1, source_target_pairs={{0,24},{8,0},{16,8},{24,16},{32,56},{40,32},{48,40},{56,48},{64,88... | collective-permute-start | bytes 393224 | tf_op jit(solution)/shard_map/ppermute | solution.py:34
  33.6 14.3 %collective-permute-start.1 = (f32[256,128]{1,0:T(8,128)S(1)}, f32[256,128]{1,0:T(8,128)S(1)}, u32[]{:S(2)}, u32[]{:S(2)}) collective-permute-start(f32[256,128]{1,0:T(8,128)S(1)} %get-tuple-element.52), channel_id=1, source_target_pairs={{0,8},{8,16},{16,24},{24,0},{32,40},{40,48},{48,56},{56,32},{64,72... | collective-permute-start | bytes 393224 | tf_op jit(solution)/shard_map/ppermute | solution.py:34
  37.3 10.7 %collective-permute-start.3 = (f32[256,128]{1,0:T(8,128)S(1)}, f32[256,128]{1,0:T(8,128)S(1)}, u32[]{:S(2)}, u32[]{:S(2)}) collective-permute-start(f32[256,128]{1,0:T(8,128)S(1)} %get-tuple-element.52), channel_id=1, source_target_pairs={{0,16},{8,24},{16,0},{24,8},{32,48},{40,56},{48,32},{56,40},{64,80... | collective-permute-start | bytes 393224 | tf_op jit(solution)/shard_map/ppermute | solution.py:34
  40.4 17.9 %collective-permute-start.24 = (f32[1,512,128]{2,1,0:T(8,128)S(1)}, f32[1,512,128]{2,1,0:T(8,128)S(1)}, u32[]{:S(2)}, u32[]{:S(2)}) collective-permute-start(f32[1,512,128]{2,1,0:T(8,128)S(1)} %collective-permute-done.20.refs_18_), channel_id=1, source_target_pairs={{0,2},{1,3},{2,4},{3,5},{4,6},{5,7},{6,0},{7,1},{8,10},{9,11},{10,... | collective-permute-start | bytes 786440 | tf_op jit(solution)/shard_map/ppermute | solution.py:34
  40.5 14.9 %collective-permute-start.11 = (f32[256,128]{1,0:T(8,128)S(1)}, f32[256,128]{1,0:T(8,128)S(1)}, u32[]{:S(2)}, u32[]{:S(2)}) collective-permute-start(f32[256,128]{1,0:T(8,128)S(1)} %get-tuple-element.51), channel_id=1, source_target_pairs={{0,96},{8,104},{16,112},{24,120},{32,0},{40,8},{48,16},{56,24},{64... | collective-permute-start | bytes 393224 | tf_op jit(solution)/shard_map/ppermute | solution.py:34
  48.0 7.5 %collective-permute-start.10 = (f32[256,128]{1,0:T(8,128)S(1)}, f32[256,128]{1,0:T(8,128)S(1)}, u32[]{:S(2)}, u32[]{:S(2)}) collective-permute-start(f32[256,128]{1,0:T(8,128)S(1)} %get-tuple-element.51), channel_id=1, source_target_pairs={{0,32},{8,40},{16,48},{24,56},{32,64},{40,72},{48,80},{56,88},{64,... | collective-permute-start | bytes 393224 | tf_op jit(solution)/shard_map/ppermute | solution.py:34
  48.0 10.3 %collective-permute-start.12 = (f32[256,128]{1,0:T(8,128)S(1)}, f32[256,128]{1,0:T(8,128)S(1)}, u32[]{:S(2)}, u32[]{:S(2)}) collective-permute-start(f32[256,128]{1,0:T(8,128)S(1)} %get-tuple-element.51), channel_id=1, source_target_pairs={{0,64},{8,72},{16,80},{24,88},{32,96},{40,104},{48,112},{56,120},{... | collective-permute-start | bytes 393224 | tf_op jit(solution)/shard_map/ppermute | solution.py:34
  53.9 7.2 %collective-permute-start.23 = (f32[1,512,128]{2,1,0:T(8,128)S(1)}, f32[1,512,128]{2,1,0:T(8,128)S(1)}, u32[]{:S(2)}, u32[]{:S(2)}) collective-permute-start(f32[1,512,128]{2,1,0:T(8,128)S(1)} %collective-permute-done.19.refs_17_), channel_id=1, source_target_pairs={{0,6},{1,7},{2,0},{3,1},{4,2},{5,3},{6,4},{7,5},{8,14},{9,15},{10,... | collective-permute-start | bytes 786440 | tf_op jit(solution)/shard_map/ppermute | solution.py:34
  55.5 7.3 %collective-permute-start.21 = (f32[1,512,128]{2,1,0:T(8,128)S(1)}, f32[1,512,128]{2,1,0:T(8,128)S(1)}, u32[]{:S(2)}, u32[]{:S(2)}) collective-permute-start(f32[1,512,128]{2,1,0:T(8,128)S(1)} %collective-permute-done.19.refs_17_), channel_id=1, source_target_pairs={{0,2},{1,3},{2,4},{3,5},{4,6},{5,7},{6,0},{7,1},{8,10},{9,11},{10,... | collective-permute-start | bytes 786440 | tf_op jit(solution)/shard_map/ppermute | solution.py:34
  55.5 8.1 %collective-permute-start.7 = (f32[2,256,128]{2,1,0:T(8,128)S(1)}, f32[2,256,128]{2,1,0:T(8,128)S(1)}, u32[]{:S(2)}, u32[]{:S(2)}) collective-permute-start(f32[2,256,128]{2,1,0:T(8,128)S(1)} %pad_maximum_fusion.1.refs_1_), channel_id=1, source_target_pairs={{0,96},{8,104},{16,112},{24,120},{32,0},{40,8},{48,16},{56,24},{64... | collective-permute-start | bytes 786440 | tf_op jit(solution)/shard_map/ppermute | solution.py:34
  58.3 7.5 %collective-permute-start.5 = (f32[2,256,128]{2,1,0:T(8,128)S(1)}, f32[2,256,128]{2,1,0:T(8,128)S(1)}, u32[]{:S(2)}, u32[]{:S(2)}) collective-permute-start(f32[2,256,128]{2,1,0:T(8,128)S(1)} %pad_maximum_fusion.1.refs_1_), channel_id=1, source_target_pairs={{0,32},{8,40},{16,48},{24,56},{32,64},{40,72},{48,80},{56,88},{64,... | collective-permute-start | bytes 786440 | tf_op jit(solution)/shard_map/ppermute | solution.py:34
  58.3 8.8 %collective-permute-start.6 = (f32[2,256,128]{2,1,0:T(8,128)S(1)}, f32[2,256,128]{2,1,0:T(8,128)S(1)}, u32[]{:S(2)}, u32[]{:S(2)}) collective-permute-start(f32[2,256,128]{2,1,0:T(8,128)S(1)} %pad_maximum_fusion.refs_0_), channel_id=1, source_target_pairs={{0,96},{8,104},{16,112},{24,120},{32,0},{40,8},{48,16},{56,24},{64... | collective-permute-start | bytes 786440 | tf_op jit(solution)/shard_map/ppermute | solution.py:34
  61.1 10.4 %collective-permute-start.4 = (f32[2,256,128]{2,1,0:T(8,128)S(1)}, f32[2,256,128]{2,1,0:T(8,128)}, u32[]{:S(2)}, u32[]{:S(2)}) collective-permute-start(f32[2,256,128]{2,1,0:T(8,128)S(1)} %pad_maximum_fusion.refs_0_), channel_id=1, source_target_pairs={{0,32},{8,40},{16,48},{24,56},{32,64},{40,72},{48,80},{56,88},{64,... | collective-permute-start | bytes 786440 | tf_op jit(solution)/shard_map/ppermute | solution.py:34
  63.5 9.2 %collective-permute-start.16 = (f32[2,256,128]{2,1,0:T(8,128)S(1)}, f32[2,256,128]{2,1,0:T(8,128)}, u32[]{:S(2)}, u32[]{:S(2)}) collective-permute-start(f32[2,256,128]{2,1,0:T(8,128)S(1)} %pad_maximum_fusion.3.refs_9_), channel_id=1, source_target_pairs={{0,24},{8,0},{16,8},{24,16},{32,56},{40,32},{48,40},{56,48},{64,88... | collective-permute-start | bytes 786440 | tf_op jit(solution)/shard_map/ppermute | solution.py:34
  63.6 9.9 %collective-permute-start.14 = (f32[2,256,128]{2,1,0:T(8,128)S(1)}, f32[2,256,128]{2,1,0:T(8,128)}, u32[]{:S(2)}, u32[]{:S(2)}) collective-permute-start(f32[2,256,128]{2,1,0:T(8,128)S(1)} %pad_maximum_fusion.3.refs_9_), channel_id=1, source_target_pairs={{0,8},{8,16},{16,24},{24,0},{32,40},{40,48},{48,56},{56,32},{64,72... | collective-permute-start | bytes 786440 | tf_op jit(solution)/shard_map/ppermute | solution.py:34
  66.5 8.3 %collective-permute-start.15 = (f32[2,256,128]{2,1,0:T(8,128)S(1)}, f32[2,256,128]{2,1,0:T(8,128)}, u32[]{:S(2)}, u32[]{:S(2)}) collective-permute-start(f32[2,256,128]{2,1,0:T(8,128)S(1)} %pad_maximum_fusion.2.refs_8_), channel_id=1, source_target_pairs={{0,24},{8,0},{16,8},{24,16},{32,56},{40,32},{48,40},{56,48},{64,88... | collective-permute-start | bytes 786440 | tf_op jit(solution)/shard_map/ppermute | solution.py:34
  67.8 9.6 %collective-permute-start.13 = (f32[2,256,128]{2,1,0:T(8,128)S(1)}, f32[2,256,128]{2,1,0:T(8,128)}, u32[]{:S(2)}, u32[]{:S(2)}) collective-permute-start(f32[2,256,128]{2,1,0:T(8,128)S(1)} %pad_maximum_fusion.2.refs_8_), channel_id=1, source_target_pairs={{0,8},{8,16},{16,24},{24,0},{32,40},{40,48},{48,56},{56,32},{64,72... | collective-permute-start | bytes 786440 | tf_op jit(solution)/shard_map/ppermute | solution.py:34
  71.5 6.0 %collective-permute-start.25 = (f32[1,512,128]{2,1,0:T(8,128)}, f32[1,512,128]{2,1,0:T(8,128)S(1)}, u32[]{:S(2)}, u32[]{:S(2)}) collective-permute-start(f32[1,512,128]{2,1,0:T(8,128)} %copy-done.3), channel_id=1, source_target_pairs={{0,6},{1,7},{2,0},{3,1},{4,2},{5,3},{6,4},{7,5},{8,14},{9,15},{10,... | collective-permute-start | bytes 786440 | tf_op jit(solution)/shard_map/ppermute | solution.py:34
  72.7 5.8 %collective-permute-start.9 = (f32[2,256,128]{2,1,0:T(8,128)}, f32[2,256,128]{2,1,0:T(8,128)S(1)}, u32[]{:S(2)}, u32[]{:S(2)}) collective-permute-start(f32[2,256,128]{2,1,0:T(8,128)} %copy-done.7), channel_id=1, source_target_pairs={{0,96},{8,104},{16,112},{24,120},{32,0},{40,8},{48,16},{56,24},{64... | collective-permute-start | bytes 786440 | tf_op jit(solution)/shard_map/ppermute | solution.py:34
  73.6 6.6 %collective-permute-start.8 = (f32[2,256,128]{2,1,0:T(8,128)}, f32[2,256,128]{2,1,0:T(8,128)S(1)}, u32[]{:S(2)}, u32[]{:S(2)}) collective-permute-start(f32[2,256,128]{2,1,0:T(8,128)} %collective-permute-done.4.refs_2_), channel_id=1, source_target_pairs={{0,32},{8,40},{16,48},{24,56},{32,64},{40,72},{48,80},{56,88},{64,... | collective-permute-start | bytes 786440 | tf_op jit(solution)/shard_map/ppermute | solution.py:34
  74.8 5.7 %collective-permute-start.18 = (f32[2,256,128]{2,1,0:T(8,128)}, f32[2,256,128]{2,1,0:T(8,128)S(1)}, u32[]{:S(2)}, u32[]{:S(2)}) collective-permute-start(f32[2,256,128]{2,1,0:T(8,128)} %collective-permute-done.16.refs_13_), channel_id=1, source_target_pairs={{0,24},{8,0},{16,8},{24,16},{32,56},{40,32},{48,40},{56,48},{64,88... | collective-permute-start | bytes 786440 | tf_op jit(solution)/shard_map/ppermute | solution.py:34
  77.4 6.9 %collective-permute-start.17 = (f32[2,256,128]{2,1,0:T(8,128)}, f32[2,256,128]{2,1,0:T(8,128)S(1)}, u32[]{:S(2)}, u32[]{:S(2)}) collective-permute-start(f32[2,256,128]{2,1,0:T(8,128)} %collective-permute-done.13.refs_10_), channel_id=1, source_target_pairs={{0,8},{8,16},{16,24},{24,0},{32,40},{40,48},{48,56},{56,32},{64,72... | collective-permute-start | bytes 786440 | tf_op jit(solution)/shard_map/ppermute | solution.py:34
  77.5 29.2 %copy-start.1 = (s32[4,16]{1,0:T(4,128)}, s32[4,16]{1,0:T(4,128)S(1)}, u32[]{:S(2)}) copy-start(s32[4,16]{1,0:T(4,128)S(1)} %pad_add_fusion.order.refs_0_) | copy-start | bytes 772
  106.6 7.5 %collective-permute-start.26 = (f32[4,64,1024]{2,1,0:T(8,128)S(1)}, f32[4,64,1024]{2,1,0:T(8,128)S(1)}, u32[]{:S(2)}, u32[]{:S(2)}) collective-permute-start(f32[4,64,1024]{2,1,0:T(8,128)S(1)} %get-tuple-element.18), channel_id=1, source_target_pairs={{0,1},{1,0},{2,3},{3,2},{4,5},{5,4},{6,7},{7,6},{8,9},{9,8},{10,11... | collective-permute-start | bytes 3145736 | tf_op jit(solution)/shard_map/ppermute | solution.py:38
  114.4 13.7 %collective-permute-start.28 = (f32[64,1024]{1,0:T(8,128)S(1)}, f32[64,1024]{1,0:T(8,128)S(1)}, u32[]{:S(2)}, u32[]{:S(2)}) collective-permute-start(f32[64,1024]{1,0:T(8,128)S(1)} %get-tuple-element.41), channel_id=1, source_target_pairs={{0,32},{1,56},{2,64},{3,88},{4,96},{5,120},{6,0},{7,24},{8,40},{9,... | collective-permute-start | bytes 786440 | tf_op jit(solution)/shard_map/ppermute | solution.py:56
  116.3 11.8 %collective-permute-start.30 = (f32[64,1024]{1,0:T(8,128)S(1)}, f32[64,1024]{1,0:T(8,128)S(1)}, u32[]{:S(2)}, u32[]{:S(2)}) collective-permute-start(f32[64,1024]{1,0:T(8,128)S(1)} %get-tuple-element.42), channel_id=1, source_target_pairs={{0,96},{1,120},{2,0},{3,24},{4,32},{5,56},{6,64},{7,88},{8,104},{9... | collective-permute-start | bytes 786440 | tf_op jit(solution)/shard_map/ppermute | solution.py:56
  120.8 12.8 %collective-permute-start.29 = (f32[64,1024]{1,0:T(8,128)S(1)}, f32[64,1024]{1,0:T(8,128)S(1)}, u32[]{:S(2)}, u32[]{:S(2)}) collective-permute-start(f32[64,1024]{1,0:T(8,128)S(1)} %get-tuple-element.43), channel_id=1, source_target_pairs={{0,64},{1,88},{2,96},{3,120},{4,0},{5,24},{6,32},{7,56},{8,72},{9,... | collective-permute-start | bytes 786440 | tf_op jit(solution)/shard_map/ppermute | solution.py:56
  124.2 9.4 %collective-permute-start.27 = (f32[64,1024]{1,0:T(8,128)S(1)}, f32[64,1024]{1,0:T(8,128)S(1)}, u32[]{:S(2)}, u32[]{:S(2)}) collective-permute-start(f32[64,1024]{1,0:T(8,128)S(1)} %get-tuple-element.44), channel_id=1, source_target_pairs={{0,0},{1,24},{2,32},{3,56},{4,64},{5,88},{6,96},{7,120},{8,8},{9,1... | collective-permute-start | bytes 786440 | tf_op jit(solution)/shard_map/ppermute | solution.py:56
  133.7 8.3 %collective-permute-start.32 = (f32[32,1024]{1,0:T(8,128)S(1)}, f32[32,1024]{1,0:T(8,128)S(1)}, u32[]{:S(2)}, u32[]{:S(2)}) collective-permute-start(f32[32,1024]{1,0:T(8,128)S(1)} %get-tuple-element.48), channel_id=1, source_target_pairs={{0,24},{8,0},{16,8},{24,16},{32,56},{40,32},{48,40},{56,48},{64,88... | collective-permute-start | bytes 393224 | tf_op jit(solution)/shard_map/ppermute | solution.py:34
  135.7 14.8 %collective-permute-start.33 = (f32[32,1024]{1,0:T(8,128)S(1)}, f32[32,1024]{1,0:T(8,128)S(1)}, u32[]{:S(2)}, u32[]{:S(2)}) collective-permute-start(f32[32,1024]{1,0:T(8,128)S(1)} %get-tuple-element.48), channel_id=1, source_target_pairs={{0,16},{8,24},{16,0},{24,8},{32,48},{40,56},{48,32},{56,40},{64,80... | collective-permute-start | bytes 393224 | tf_op jit(solution)/shard_map/ppermute | solution.py:34
  135.7 14.9 %collective-permute-start.31 = (f32[32,1024]{1,0:T(8,128)S(1)}, f32[32,1024]{1,0:T(8,128)S(1)}, u32[]{:S(2)}, u32[]{:S(2)}) collective-permute-start(f32[32,1024]{1,0:T(8,128)S(1)} %get-tuple-element.48), channel_id=1, source_target_pairs={{0,8},{8,16},{16,24},{24,0},{32,40},{40,48},{48,56},{56,32},{64,72... | collective-permute-start | bytes 393224 | tf_op jit(solution)/shard_map/ppermute | solution.py:34
  136.4 15.8 %collective-permute-start.41 = (f32[32,1024]{1,0:T(8,128)S(1)}, f32[32,1024]{1,0:T(8,128)S(1)}, u32[]{:S(2)}, u32[]{:S(2)}) collective-permute-start(f32[32,1024]{1,0:T(8,128)S(1)} %get-tuple-element.47), channel_id=1, source_target_pairs={{0,96},{8,104},{16,112},{24,120},{32,0},{40,8},{48,16},{56,24},{64... | collective-permute-start | bytes 393224 | tf_op jit(solution)/shard_map/ppermute | solution.py:34
  141.9 12.2 %collective-permute-start.40 = (f32[32,1024]{1,0:T(8,128)S(1)}, f32[32,1024]{1,0:T(8,128)S(1)}, u32[]{:S(2)}, u32[]{:S(2)}) collective-permute-start(f32[32,1024]{1,0:T(8,128)S(1)} %get-tuple-element.47), channel_id=1, source_target_pairs={{0,32},{8,40},{16,48},{24,56},{32,64},{40,72},{48,80},{56,88},{64,... | collective-permute-start | bytes 393224 | tf_op jit(solution)/shard_map/ppermute | solution.py:34
  141.9 11.6 %collective-permute-start.42 = (f32[32,1024]{1,0:T(8,128)S(1)}, f32[32,1024]{1,0:T(8,128)S(1)}, u32[]{:S(2)}, u32[]{:S(2)}) collective-permute-start(f32[32,1024]{1,0:T(8,128)S(1)} %get-tuple-element.47), channel_id=1, source_target_pairs={{0,64},{8,72},{16,80},{24,88},{32,96},{40,104},{48,112},{56,120},{... | collective-permute-start | bytes 393224 | tf_op jit(solution)/shard_map/ppermute | solution.py:34
  150.6 26.8 %copy-start.18 = (f32[2,32,1024]{2,1,0:T(8,128)}, f32[2,32,1024]{2,1,0:T(8,128)S(1)}, u32[]{:S(2)}) copy-start(f32[2,32,1024]{2,1,0:T(8,128)S(1)} %pad_maximum_fusion.5.refs_2_) | copy-start | bytes 786436
  150.6 6.8 %collective-permute-start.37 = (f32[2,32,1024]{2,1,0:T(8,128)S(1)}, f32[2,32,1024]{2,1,0:T(8,128)S(1)}, u32[]{:S(2)}, u32[]{:S(2)}) collective-permute-start(f32[2,32,1024]{2,1,0:T(8,128)S(1)} %pad_maximum_fusion.5.refs_2_), channel_id=1, source_target_pairs={{0,96},{8,104},{16,112},{24,120},{32,0},{40,8},{48,16},{56,24},{64... | collective-permute-start | bytes 786440 | tf_op jit(solution)/shard_map/ppermute | solution.py:34
  150.7 7.8 %collective-permute-start.35 = (f32[2,32,1024]{2,1,0:T(8,128)S(1)}, f32[2,32,1024]{2,1,0:T(8,128)S(1)}, u32[]{:S(2)}, u32[]{:S(2)}) collective-permute-start(f32[2,32,1024]{2,1,0:T(8,128)S(1)} %pad_maximum_fusion.5.refs_2_), channel_id=1, source_target_pairs={{0,32},{8,40},{16,48},{24,56},{32,64},{40,72},{48,80},{56,88},{64,... | collective-permute-start | bytes 786440 | tf_op jit(solution)/shard_map/ppermute | solution.py:34
  152.1 25.2 %copy-start.19 = (f32[2,32,1024]{2,1,0:T(8,128)}, f32[2,32,1024]{2,1,0:T(8,128)S(1)}, u32[]{:S(2)}) copy-start(f32[2,32,1024]{2,1,0:T(8,128)S(1)} %pad_maximum_fusion.4.refs_1_) | copy-start | bytes 786436
  152.2 10.6 %collective-permute-start.36 = (f32[2,32,1024]{2,1,0:T(8,128)S(1)}, f32[2,32,1024]{2,1,0:T(8,128)S(1)}, u32[]{:S(2)}, u32[]{:S(2)}) collective-permute-start(f32[2,32,1024]{2,1,0:T(8,128)S(1)} %pad_maximum_fusion.4.refs_1_), channel_id=1, source_target_pairs={{0,96},{8,104},{16,112},{24,120},{32,0},{40,8},{48,16},{56,24},{64... | collective-permute-start | bytes 786440 | tf_op jit(solution)/shard_map/ppermute | solution.py:34
  153.5 13.0 %collective-permute-start.34 = (f32[2,32,1024]{2,1,0:T(8,128)S(1)}, f32[2,32,1024]{2,1,0:T(8,128)S(1)}, u32[]{:S(2)}, u32[]{:S(2)}) collective-permute-start(f32[2,32,1024]{2,1,0:T(8,128)S(1)} %pad_maximum_fusion.4.refs_1_), channel_id=1, source_target_pairs={{0,32},{8,40},{16,48},{24,56},{32,64},{40,72},{48,80},{56,88},{64,... | collective-permute-start | bytes 786440 | tf_op jit(solution)/shard_map/ppermute | solution.py:34
  154.1 13.9 %collective-permute-start.46 = (f32[2,32,1024]{2,1,0:T(8,128)S(1)}, f32[2,32,1024]{2,1,0:T(8,128)S(1)}, u32[]{:S(2)}, u32[]{:S(2)}) collective-permute-start(f32[2,32,1024]{2,1,0:T(8,128)S(1)} %pad_maximum_fusion.7.refs_10_), channel_id=1, source_target_pairs={{0,24},{8,0},{16,8},{24,16},{32,56},{40,32},{48,40},{56,48},{64,88... | collective-permute-start | bytes 786440 | tf_op jit(solution)/shard_map/ppermute | solution.py:34
  157.4 10.6 %collective-permute-start.44 = (f32[2,32,1024]{2,1,0:T(8,128)S(1)}, f32[2,32,1024]{2,1,0:T(8,128)S(1)}, u32[]{:S(2)}, u32[]{:S(2)}) collective-permute-start(f32[2,32,1024]{2,1,0:T(8,128)S(1)} %pad_maximum_fusion.7.refs_10_), channel_id=1, source_target_pairs={{0,8},{8,16},{16,24},{24,0},{32,40},{40,48},{48,56},{56,32},{64,72... | collective-permute-start | bytes 786440 | tf_op jit(solution)/shard_map/ppermute | solution.py:34
  158.5 11.8 %collective-permute-start.43 = (f32[2,32,1024]{2,1,0:T(8,128)S(1)}, f32[2,32,1024]{2,1,0:T(8,128)}, u32[]{:S(2)}, u32[]{:S(2)}) collective-permute-start(f32[2,32,1024]{2,1,0:T(8,128)S(1)} %pad_maximum_fusion.6.refs_9_), channel_id=1, source_target_pairs={{0,8},{8,16},{16,24},{24,0},{32,40},{40,48},{48,56},{56,32},{64,72... | collective-permute-start | bytes 786440 | tf_op jit(solution)/shard_map/ppermute | solution.py:34
  162.8 8.2 %collective-permute-start.45 = (f32[2,32,1024]{2,1,0:T(8,128)S(1)}, f32[2,32,1024]{2,1,0:T(8,128)}, u32[]{:S(2)}, u32[]{:S(2)}) collective-permute-start(f32[2,32,1024]{2,1,0:T(8,128)S(1)} %pad_maximum_fusion.6.refs_9_), channel_id=1, source_target_pairs={{0,24},{8,0},{16,8},{24,16},{32,56},{40,32},{48,40},{56,48},{64,88... | collective-permute-start | bytes 786440 | tf_op jit(solution)/shard_map/ppermute | solution.py:34
  166.5 5.7 %collective-permute-start.39 = (f32[2,32,1024]{2,1,0:T(8,128)S(1)}, f32[2,32,1024]{2,1,0:T(8,128)}, u32[]{:S(2)}, u32[]{:S(2)}) collective-permute-start(f32[2,32,1024]{2,1,0:T(8,128)S(1)} %collective-permute-done.37.refs_6_), channel_id=1, source_target_pairs={{0,96},{8,104},{16,112},{24,120},{32,0},{40,8},{48,16},{56,24},{64... | collective-permute-start | bytes 786440 | tf_op jit(solution)/shard_map/ppermute | solution.py:34
  168.0 6.9 %collective-permute-start.38 = (f32[2,32,1024]{2,1,0:T(8,128)S(1)}, f32[2,32,1024]{2,1,0:T(8,128)}, u32[]{:S(2)}, u32[]{:S(2)}) collective-permute-start(f32[2,32,1024]{2,1,0:T(8,128)S(1)} %collective-permute-done.34.refs_3_), channel_id=1, source_target_pairs={{0,32},{8,40},{16,48},{24,56},{32,64},{40,72},{48,80},{56,88},{64,... | collective-permute-start | bytes 786440 | tf_op jit(solution)/shard_map/ppermute | solution.py:34
  168.1 8.4 %collective-permute-start.48 = (f32[2,32,1024]{2,1,0:T(8,128)S(1)}, f32[2,32,1024]{2,1,0:T(8,128)}, u32[]{:S(2)}, u32[]{:S(2)}) collective-permute-start(f32[2,32,1024]{2,1,0:T(8,128)S(1)} %collective-permute-done.46.refs_14_), channel_id=1, source_target_pairs={{0,24},{8,0},{16,8},{24,16},{32,56},{40,32},{48,40},{56,48},{64,88... | collective-permute-start | bytes 786440 | tf_op jit(solution)/shard_map/ppermute | solution.py:34
  170.3 7.0 %collective-permute-start.47 = (f32[2,32,1024]{2,1,0:T(8,128)}, f32[2,32,1024]{2,1,0:T(8,128)}, u32[]{:S(2)}, u32[]{:S(2)}) collective-permute-start(f32[2,32,1024]{2,1,0:T(8,128)} %collective-permute-done.43.refs_11_), channel_id=1, source_target_pairs={{0,8},{8,16},{16,24},{24,0},{32,40},{40,48},{48,56},{56,32},{64,72... | collective-permute-start | bytes 786440 | tf_op jit(solution)/shard_map/ppermute | solution.py:34
  191.6 7.0 %collective-permute-start.49 = (f32[2,1024,128]{2,1,0:T(8,128)}, f32[2,1024,128]{2,1,0:T(8,128)S(1)}, u32[]{:S(2)}, u32[]{:S(2)}) collective-permute-start(f32[2,1024,128]{2,1,0:T(8,128)} %get-tuple-element.22), channel_id=1, source_target_pairs={{0,1},{1,0},{2,3},{3,2},{4,5},{5,4},{6,7},{7,6},{8,9},{9,8},{10,11... | collective-permute-start | bytes 3145736 | tf_op jit(solution)/shard_map/ppermute | solution.py:38
  196.8 16.3 %collective-permute-start.52 = (f32[2,1024,128]{2,1,0:T(8,128)}, f32[2,1024,128]{2,1,0:T(8,128)S(1)}, u32[]{:S(2)}, u32[]{:S(2)}) collective-permute-start(f32[2,1024,128]{2,1,0:T(8,128)} %get-tuple-element.28), channel_id=1, source_target_pairs={{0,1},{1,0},{2,3},{3,2},{4,5},{5,4},{6,7},{7,6},{8,9},{9,8},{10,11... | collective-permute-start | bytes 3145736 | tf_op jit(solution)/shard_map/ppermute | solution.py:38
  212.6 15.2 %collective-permute-start.51 = (f32[2,1024,128]{2,1,0:T(8,128)}, f32[2,1024,128]{2,1,0:T(8,128)S(1)}, u32[]{:S(2)}, u32[]{:S(2)}) collective-permute-start(f32[2,1024,128]{2,1,0:T(8,128)} %get-tuple-element.26), channel_id=1, source_target_pairs={{0,1},{1,0},{2,3},{3,2},{4,5},{5,4},{6,7},{7,6},{8,9},{9,8},{10,11... | collective-permute-start | bytes 3145736 | tf_op jit(solution)/shard_map/ppermute | solution.py:38
  213.2 14.6 %collective-permute-start.53 = (f32[1024,128]{1,0:T(8,128)S(1)}, f32[1024,128]{1,0:T(8,128)S(1)}, u32[]{:S(2)}, u32[]{:S(2)}) collective-permute-start(f32[1024,128]{1,0:T(8,128)S(1)} %get-tuple-element.37), channel_id=1, source_target_pairs={{0,2},{1,3},{2,4},{3,5},{4,6},{5,7},{6,0},{7,1},{8,10},{9,11},{10,... | collective-permute-start | bytes 1572872 | tf_op jit(solution)/shard_map/ppermute | solution.py:34
  214.6 13.3 %collective-permute-start.57 = (f32[1024,128]{1,0:T(8,128)S(1)}, f32[1024,128]{1,0:T(8,128)S(1)}, u32[]{:S(2)}, u32[]{:S(2)}) collective-permute-start(f32[1024,128]{1,0:T(8,128)S(1)} %get-tuple-element.38), channel_id=1, source_target_pairs={{0,6},{1,7},{2,0},{3,1},{4,2},{5,3},{6,4},{7,5},{8,14},{9,15},{10,... | collective-permute-start | bytes 1572872 | tf_op jit(solution)/shard_map/ppermute | solution.py:34
  215.9 23.8 %collective-permute-start.50 = (f32[2,1024,128]{2,1,0:T(8,128)S(1)}, f32[2,1024,128]{2,1,0:T(8,128)S(1)}, u32[]{:S(2)}, u32[]{:S(2)}) collective-permute-start(f32[2,1024,128]{2,1,0:T(8,128)S(1)} %copy-done.23), channel_id=1, source_target_pairs={{0,1},{1,0},{2,3},{3,2},{4,5},{5,4},{6,7},{7,6},{8,9},{9,8},{10,11... | collective-permute-start | bytes 3145736 | tf_op jit(solution)/shard_map/ppermute | solution.py:38
  216.6 22.4 %collective-permute-start.56 = (f32[1024,128]{1,0:T(8,128)S(1)}, f32[1024,128]{1,0:T(8,128)S(1)}, u32[]{:S(2)}, u32[]{:S(2)}) collective-permute-start(f32[1024,128]{1,0:T(8,128)S(1)} %copy-done.17), channel_id=1, source_target_pairs={{0,2},{1,3},{2,4},{3,5},{4,6},{5,7},{6,0},{7,1},{8,10},{9,11},{10,... | collective-permute-start | bytes 1572872 | tf_op jit(solution)/shard_map/ppermute | solution.py:34
  227.8 11.9 %collective-permute-start.55 = (f32[1024,128]{1,0:T(8,128)S(1)}, f32[1024,128]{1,0:T(8,128)S(1)}, u32[]{:S(2)}, u32[]{:S(2)}) collective-permute-start(f32[1024,128]{1,0:T(8,128)S(1)} %copy-done.16), channel_id=1, source_target_pairs={{0,6},{1,7},{2,0},{3,1},{4,2},{5,3},{6,4},{7,5},{8,14},{9,15},{10,... | collective-permute-start | bytes 1572872 | tf_op jit(solution)/shard_map/ppermute | solution.py:34
  228.1 22.2 %collective-permute-start.54 = (f32[1024,128]{1,0:T(8,128)S(1)}, f32[1024,128]{1,0:T(8,128)S(1)}, u32[]{:S(2)}, u32[]{:S(2)}) collective-permute-start(f32[1024,128]{1,0:T(8,128)S(1)} %get-tuple-element.35), channel_id=1, source_target_pairs={{0,2},{1,3},{2,4},{3,5},{4,6},{5,7},{6,0},{7,1},{8,10},{9,11},{10,... | collective-permute-start | bytes 1572872 | tf_op jit(solution)/shard_map/ppermute | solution.py:34
  229.6 21.4 %collective-permute-start.58 = (f32[1024,128]{1,0:T(8,128)S(1)}, f32[1024,128]{1,0:T(8,128)S(1)}, u32[]{:S(2)}, u32[]{:S(2)}) collective-permute-start(f32[1024,128]{1,0:T(8,128)S(1)} %get-tuple-element.36), channel_id=1, source_target_pairs={{0,6},{1,7},{2,0},{3,1},{4,2},{5,3},{6,4},{7,5},{8,14},{9,15},{10,... | collective-permute-start | bytes 1572872 | tf_op jit(solution)/shard_map/ppermute | solution.py:34
  (26 other events, 213.7 us)
